TPU v7x, 256 devices: a whole 4x4x8 slice. The times are simulated.
256 devices in a mesh: exc: 16 (over y, z_hi), space: 16 (over z_lo, x, core).
Axes of the slice: x: 4, y: 4, z: 8 (z_hi: 4, z_lo: 2; z = z_hi * 2 + z_lo), core: 2. Of those that a mesh axis runs over, the one named last changes fastest.
Arguments:
- adj_e: float32 [16, 192, 4096], P('exc', None, 'space'), may hold values from -6 to 6
- adj_h: float32 [16, 192, 4096], P('exc', None, 'space'), may hold values from -6 to 6
- adj_j: float32 [16, 192, 4096], P('exc', None, 'space'), may hold values from -6 to 6
- fwd_e: bfloat16 [16, 5, 192, 4096], P('exc', None, None, 'space'), may hold values from -6 to 6
- inv_eps: float32 [64, 4096], P(None, 'space'), may hold values from 0.08 to 1
- drude_weight: float32 [64, 4096], P(None, 'space'), may hold values from 0.5 to 20
- neighbor: int32 [6, 4096], P(None, 'space'), may hold values from -1 to 4095, as said below
- design_map: int32 [4096], P('space'), may hold values from 0 to 2047, as said below
- port_elems: int32 [16, 2048], P('exc', 'space'), may hold values from 0 to 4095, as said below
- port_profile: float32 [16, 192, 2048], P('exc', None, 'space'), may hold values from -48 to 48
Outputs:
- adj_e_out: float32 [16, 192, 4096], P('exc', None, 'space')
- adj_h_out: float32 [16, 192, 4096], P('exc', None, 'space')
- grad_eps: float32 [64, 2048], P(None, ('space', 'exc'))
- grad_drude: float32 [64, 2048], P(None, ('space', 'exc'))
Inputs may be any that keep to these rules, and one draw needn't show every extreme that they name: neighbor[f, e] is the element across face f (x-, x+, y-, y+, z-, z+) of element e, which touches it with its opposite face; it is -1 across the x- face of the first and the x+ face of the last element layer. Elements are stored layer by layer in layers of 128 elements along x, so each block of 256 elements is 2 whole layers; a y or z neighbour lies in the same layer (periodic in y and z), an x neighbour in the adjacent layer. `design_map`: an element of the b-th block of 256 elements maps to a pixel of the b-th block of 128 pixels, and every pixel holds exactly two elements. `port_elems`: columns b * 128 to (b + 1) * 128 - 1 of each row hold 128 distinct elements of the b-th block of 256 elements.
All inputs are finite; a program needn't handle non-finite values.
Results may differ from a plain program's by a relative error of at most 0.00035.
Values sent between devices are 32-bit elements; how exact they have to be, the bound alone decides.
A program may use at most 64 MiB of HBM per device.

v0:
```python
import jax
import jax.numpy as jnp
import numpy as np
from jax import lax
from jax.sharding import PartitionSpec as P

NODES = 64
STEPS = 4
LAYER = 128
PIX_DEV = 128


TIME_STEP = 0.025
DAMPING = 0.5


def padded(shard, sides, width):
    for axis, dim in sides:
        size, length = (lax.axis_size(axis), shard.shape[dim])
        up = [(i, (i + 1) % size) for i in range(size - 1)]
        down = [(j, i) for i, j in up]
        last = lax.slice_in_dim(shard, length - width, length, axis=dim)
        leading = lax.slice_in_dim(shard, 0, width, axis=dim)
        before = lax.ppermute(last, axis, up)
        after = lax.ppermute(leading, axis, down)
        shard = jnp.concatenate([before, shard, after], axis=dim)
    return shard


def node_tables():
    points = np.array([-1.0, -1.0 / np.sqrt(5.0), 1.0 / np.sqrt(5.0), 1.0])
    barycentric = np.array(
        [1.0 / np.prod([points[j] - points[k] for k in range(4) if k != j]) for j in range(4)]
    )
    deriv = np.zeros((4, 4))
    for row in range(4):
        for column in range(4):
            if row != column:
                deriv[row, column] = (
                    barycentric[column] / barycentric[row] / (points[row] - points[column])
                )
        deriv[row, row] = -np.sum(deriv[row])
    identity = np.eye(4)
    along_x = 2.0 * np.kron(np.kron(deriv, identity), identity)
    along_y = 2.0 * np.kron(np.kron(identity, deriv), identity)
    along_z = 2.0 * np.kron(np.kron(identity, identity), deriv)
    curl_table = np.zeros((192, 192))
    curl_table[0:64, 64:128] = -along_z
    curl_table[0:64, 128:192] = along_y
    curl_table[64:128, 0:64] = along_z
    curl_table[64:128, 128:192] = -along_x
    curl_table[128:192, 0:64] = -along_y
    curl_table[128:192, 64:128] = along_x
    numbers = np.arange(64).reshape(4, 4, 4)
    faces = np.stack(
        [
            numbers[0].ravel(),
            numbers[3].ravel(),
            numbers[:, 0].ravel(),
            numbers[:, 3].ravel(),
            numbers[:, :, 0].ravel(),
            numbers[:, :, 3].ravel(),
        ]
    )
    inner_table = np.zeros((192, 192))
    face_table = np.zeros((192, 288))
    for face in range(6):
        direction = face // 2
        sign = 1.0 if face % 2 else -1.0
        for component in range(3):
            for other in range(3):
                parity = (component - direction) * (direction - other) * (other - component) / 2.0
                if parity != 0:
                    for node in range(16):
                        value = 6.0 * sign * parity
                        face_table[
                            component * 64 + faces[face, node], face * 48 + other * 16 + node
                        ] += value
                        inner_table[
                            component * 64 + faces[face, node], other * 64 + faces[face, node]
                        ] += value
    return (curl_table, inner_table, face_table)


def face_rows(field, face):
    width = field.shape[1]
    cube = field.reshape(3, 4, 4, 4, width)
    if face == 0:
        picked = cube[:, 0]
    elif face == 1:
        picked = cube[:, 3]
    elif face == 2:
        picked = cube[:, :, 0]
    elif face == 3:
        picked = cube[:, :, 3]
    elif face == 4:
        picked = cube[:, :, :, 0]
    else:
        picked = cube[:, :, :, 3]
    return picked.reshape(48, width)


def local(
    adj_e,
    adj_h,
    adj_j,
    fwd_e,
    inv_eps,
    drude_weight,
    neighbor,
    design_map,
    port_elems,
    port_profile,
):
    curl_np, inner_np, face_np = node_tables()
    curl_table = jnp.asarray(curl_np, jnp.float32)
    inner_table = jnp.asarray(inner_np, jnp.float32)
    face_table = jnp.asarray(face_np, jnp.float32)
    count = adj_e.shape[2]
    layer = LAYER
    space_rank = lax.axis_index("space")
    offsets = neighbor - space_rank * count
    valid = (neighbor >= 0).astype(jnp.float32)
    inverse = jnp.tile(inv_eps, (3, 1))
    plasma = jnp.tile(drude_weight, (3, 1))
    source = (
        jnp.zeros((3 * NODES, count), jnp.float32)
        .at[:, port_elems[0] - space_rank * count]
        .add(port_profile[0])
    )
    pixel_index = design_map - space_rank * PIX_DEV
    pixel_table = (pixel_index[:, None] == jnp.arange(PIX_DEV, dtype=jnp.int32)[None, :]).astype(
        jnp.float32
    )
    history = fwd_e[0]

    def outer_traces(field):
        pieces = []
        wide = padded(field, (("space", 1),), layer)
        for face in range(6):
            rows = face_rows(wide, face ^ 1)
            position = jnp.clip(offsets[face] + layer, 0, count + 2 * layer - 1)
            pieces.append(jnp.take(rows, position, axis=1) * valid[face])
        return jnp.concatenate(pieces, axis=0)

    def flux_term(field):
        own = jnp.dot(
            inner_table, field, preferred_element_type=jnp.float32, precision=lax.Precision.HIGHEST
        )
        return own - jnp.dot(
            face_table,
            outer_traces(field),
            preferred_element_type=jnp.float32,
            precision=lax.Precision.HIGHEST,
        )

    electric = adj_e[0]
    magnetic = adj_h[0]
    current = adj_j[0]
    owners = lax.axis_size("exc")
    total_eps = jnp.zeros((NODES, count), jnp.float32)
    total_drude = jnp.zeros((NODES, count), jnp.float32)
    for step in range(STEPS):
        magnetic = magnetic + TIME_STEP * (
            flux_term(electric)
            - jnp.dot(
                curl_table,
                electric,
                preferred_element_type=jnp.float32,
                precision=lax.Precision.HIGHEST,
            )
        )
        current = (1.0 - TIME_STEP * DAMPING) * current + TIME_STEP * plasma * electric
        electric = electric + TIME_STEP * inverse * (
            jnp.dot(
                curl_table,
                magnetic,
                preferred_element_type=jnp.float32,
                precision=lax.Precision.HIGHEST,
            )
            - flux_term(magnetic)
            - current
            - source
        )
        before = history[step].astype(jnp.float32)
        change = history[step + 1].astype(jnp.float32) - before
        step_eps = jnp.sum((electric * change).reshape(3, NODES, count), axis=0)
        step_drude = jnp.sum((current * before).reshape(3, NODES, count), axis=0)
        total_eps = total_eps + step_eps
        total_drude = total_drude + step_drude
    stacked = jnp.concatenate([total_eps, total_drude], axis=0)
    totals = lax.psum_scatter(
        jnp.dot(
            stacked,
            pixel_table,
            preferred_element_type=jnp.float32,
            precision=lax.Precision.HIGHEST,
        ),
        "exc",
        scatter_dimension=1,
        tiled=True,
    )
    totals = totals / owners
    return (electric[None], magnetic[None], totals[:NODES], totals[NODES:])


def solution(mesh):
    return jax.shard_map(
        local,
        mesh=mesh,
        in_specs=(
            P("exc", None, "space"),
            P("exc", None, "space"),
            P("exc", None, "space"),
            P("exc", None, None, "space"),
            P(None, "space"),
            P(None, "space"),
            P(None, "space"),
            P("space"),
            P("exc", "space"),
            P("exc", None, "space"),
        ),
        out_specs=(
            P("exc", None, "space"),
            P("exc", None, "space"),
            P(None, ("space", "exc")),
            P(None, ("space", "exc")),
        ),
        check_vma=False,
    )
```

profile of v0, /device:TPU:2, one launch (start us, length us, event | category | flops | bytes accessed | tf_op | source)
XLA Modules:
  0.0 379.7 jit_solution(5304535746206592573)
XLA Ops:
  7.2 1.0 fusion.331
  8.2 1.9 collective-permute-start.1
  10.2 2.4 collective-permute-start
  18.5 1.3 scatter_custom_fusion
  22.8 1.0 fusion.268
  26.7 1.3 gather_fusion.4
  39.5 3.0 collective-permute-start.2
  42.5 2.9 collective-permute-start.3
  45.4 1.0 fusion.334
  46.4 1.0 collective-permute-done.3
  50.8 1.3 gather_fusion.8
  52.2 1.3 gather_fusion.10
  53.7 1.3 gather_fusion.11
  60.2 1.2 convert_multiply_fusion.2
  61.5 3.4 collective-permute-start.4
  64.9 2.4 collective-permute-start.5
  71.0 1.3 gather_fusion.12
  72.4 1.3 fusion.61
  73.9 1.3 gather_fusion.13
  75.5 1.3 gather_fusion.14
  78.7 1.3 gather_fusion.15
  80.1 1.1 convolution_add_fusion.29
  84.1 1.0 fusion.338
  85.1 4.4 %collective-permute-start.6 = (f32[192,128]{1,0:T(8,128)S(1)}, f32[192,128]{1,0:T(8,128)S(1)}, u32[]{:S(2)}, u32[]{:S(2)}) collective-permute-start(f32[192,128]{1,0:T(8,128)S(1)} %get-tuple-element.70), channel_id=1, source_target_pairs={{0,1},{1,2},{2,3},{3,4},{4,5},{5,6},{6,7},{7,8},{8,9},{9,10},{10,1... | collective-permute-start | bytes 294920 | tf_op jit(solution)/shard_map/ppermute | solution.py:24
  89.6 2.1 collective-permute-start.7
  91.7 1.0 fusion.337
  92.7 1.0 collective-permute-done.7
  97.0 1.3 gather_fusion.20
  98.5 1.3 gather_fusion.22
  100.0 1.3 gather_fusion.23
  101.4 1.3 gather_fusion.21
  106.6 1.2 convert_multiply_fusion.1
  107.8 5.9 %collective-permute-start.8 = (f32[192,128]{1,0:T(8,128)S(1)}, f32[192,128]{1,0:T(8,128)S(1)}, u32[]{:S(2)}, u32[]{:S(2)}) collective-permute-start(f32[192,128]{1,0:T(8,128)S(1)} %get-tuple-element.68), channel_id=1, source_target_pairs={{0,1},{1,2},{2,3},{3,4},{4,5},{5,6},{6,7},{7,8},{8,9},{9,10},{10,1... | collective-permute-start | bytes 294920 | tf_op jit(solution)/shard_map/ppermute | solution.py:24
  113.7 1.9 collective-permute-start.9
  119.4 1.3 gather_fusion.24
  120.8 1.3 fusion.59
  122.2 1.3 gather_fusion.25
  123.9 1.3 gather_fusion.26
  127.1 1.3 gather_fusion.27
  128.5 1.1 convolution_add_fusion.19
  132.5 1.0 fusion.341
  133.5 5.8 %collective-permute-start.10 = (f32[192,128]{1,0:T(8,128)S(1)}, f32[192,128]{1,0:T(8,128)S(1)}, u32[]{:S(2)}, u32[]{:S(2)}) collective-permute-start(f32[192,128]{1,0:T(8,128)S(1)} %get-tuple-element.66), channel_id=1, source_target_pairs={{0,1},{1,2},{2,3},{3,4},{4,5},{5,6},{6,7},{7,8},{8,9},{9,10},{10,1... | collective-permute-start | bytes 294920 | tf_op jit(solution)/shard_map/ppermute | solution.py:24
  139.4 2.3 collective-permute-start.11
  141.7 1.0 fusion.340
  146.8 1.3 gather_fusion.32
  148.2 1.3 gather_fusion.34
  149.7 1.3 gather_fusion.35
  155.5 1.2 convert_multiply_fusion
  157.1 6.0 %collective-permute-start.12 = (f32[192,128]{1,0:T(8,128)S(1)}, f32[192,128]{1,0:T(8,128)S(1)}, u32[]{:S(2)}, u32[]{:S(2)}) collective-permute-start(f32[192,128]{1,0:T(8,128)S(1)} %get-tuple-element.64), channel_id=1, source_target_pairs={{0,1},{1,2},{2,3},{3,4},{4,5},{5,6},{6,7},{7,8},{8,9},{9,10},{10,1... | collective-permute-start | bytes 294920 | tf_op jit(solution)/shard_map/ppermute | solution.py:24
  163.1 1.9 collective-permute-start.13
  165.7 1.5 collective-permute-done.13
  168.8 1.3 gather_fusion.36
  170.2 1.3 fusion.57
  171.6 1.3 gather_fusion.37
  173.3 1.3 gather_fusion.38
  176.5 1.3 gather_fusion.39
  177.8 1.1 convolution_add_fusion.9
  182.2 5.9 %collective-permute-start.14 = (f32[192,128]{1,0:T(8,128)S(1)}, f32[192,128]{1,0:T(8,128)S(1)}, u32[]{:S(2)}, u32[]{:S(2)}) collective-permute-start(f32[192,128]{1,0:T(8,128)S(1)} %get-tuple-element.62), channel_id=1, source_target_pairs={{0,1},{1,2},{2,3},{3,4},{4,5},{5,6},{6,7},{7,8},{8,9},{9,10},{10,1... | collective-permute-start | bytes 294920 | tf_op jit(solution)/shard_map/ppermute | solution.py:24
  188.1 2.1 collective-permute-start.15
  190.5 1.7 collective-permute-done.15
  198.1 1.3 gather_fusion.45
  202.7 1.1 fusion.47
  205.4 1.0 fusion.52
  208.4 163.0 %all-reduce.3.cloned.1.call-done = f32[128,128]{0,1:T(8,128)} async-done(((f32[128,128]{0,1:T(8,128)}), f32[128,128]{0,1:T(8,128)}) %all-reduce.3.cloned.1.call-update) | async-done | bytes 65552
  (493 shorter events, 86.5 us)
Async XLA Ops:
  7.2 364.2 %all-reduce.3.cloned.1.call-start = ((), (), s32[]{:S(2)}) async-start(), calls=%async_computation | async-start | bytes 131072
  7.2 8.6 %copy-start.2 = (f32[1,192,256]{2,1,0:T(8,128)S(1)}, f32[1,192,256]{2,1,0:T(8,128)}, u32[]{:S(2)}) copy-start(f32[1,192,256]{2,1,0:T(8,128)} %param.15) | copy-start | bytes 589828
  8.2 4.4 %copy-start.66 = (s32[6,256]{1,0:T(8,128)S(1)}, s32[6,256]{1,0:T(8,128)}, u32[]{:S(2)}) copy-start(s32[6,256]{1,0:T(8,128)} %param.21) | copy-start | bytes 18436
  8.2 17.0 %collective-permute-start.1 = (f32[192,128]{1,0:T(8,128)S(1)}, f32[192,128]{1,0:T(8,128)S(1)}, u32[]{:S(2)}, u32[]{:S(2)}) collective-permute-start(f32[192,128]{1,0:T(8,128)S(1)} %get-tuple-element.76), channel_id=1, source_target_pairs={{1,0},{2,1},{3,2},{4,3},{5,4},{6,5},{7,6},{8,7},{9,8},{10,9},{11,1... | collective-permute-start | bytes 294920 | tf_op jit(solution)/shard_map/ppermute | solution.py:25
  10.2 14.9 %collective-permute-start = (f32[192,128]{1,0:T(8,128)S(1)}, f32[192,128]{1,0:T(8,128)S(1)}, u32[]{:S(2)}, u32[]{:S(2)}) collective-permute-start(f32[192,128]{1,0:T(8,128)S(1)} %get-tuple-element.77), channel_id=1, source_target_pairs={{0,1},{1,2},{2,3},{3,4},{4,5},{5,6},{6,7},{7,8},{8,9},{9,10},{10,1... | collective-permute-start | bytes 294920 | tf_op jit(solution)/shard_map/ppermute | solution.py:24
  17.5 0.9 copy-start.55
  19.9 0.9 copy-start.11
  20.8 1.1 copy-start.10
  21.9 0.9 copy-start
  22.8 1.0 copy-start.105
  35.6 0.9 copy-start.36
  36.7 1.0 copy-start.12
  37.8 0.9 copy-start.1
  37.8 1.0 copy-start.54
  39.5 6.9 %collective-permute-start.2 = (f32[192,128]{1,0:T(8,128)S(1)}, f32[192,128]{1,0:T(8,128)S(1)}, u32[]{:S(2)}, u32[]{:S(2)}) collective-permute-start(f32[192,128]{1,0:T(8,128)S(1)} %get-tuple-element.74), channel_id=1, source_target_pairs={{0,1},{1,2},{2,3},{3,4},{4,5},{5,6},{6,7},{7,8},{8,9},{9,10},{10,1... | collective-permute-start | bytes 294920 | tf_op jit(solution)/shard_map/ppermute | solution.py:24
  42.5 4.9 %collective-permute-start.3 = (f32[192,128]{1,0:T(8,128)S(1)}, f32[192,128]{1,0:T(8,128)S(1)}, u32[]{:S(2)}, u32[]{:S(2)}) collective-permute-start(f32[192,128]{1,0:T(8,128)S(1)} %get-tuple-element.75), channel_id=1, source_target_pairs={{1,0},{2,1},{3,2},{4,3},{5,4},{6,5},{7,6},{8,7},{9,8},{10,9},{11,1... | collective-permute-start | bytes 294920 | tf_op jit(solution)/shard_map/ppermute | solution.py:25
  58.4 1.0 copy-start.18
  58.4 1.0 copy-start.52
  59.2 1.0 copy-start.14
  59.2 0.9 copy-start.97
  61.5 7.4 %collective-permute-start.4 = (f32[192,128]{1,0:T(8,128)S(1)}, f32[192,128]{1,0:T(8,128)S(1)}, u32[]{:S(2)}, u32[]{:S(2)}) collective-permute-start(f32[192,128]{1,0:T(8,128)S(1)} %get-tuple-element.72), channel_id=1, source_target_pairs={{0,1},{1,2},{2,3},{3,4},{4,5},{5,6},{6,7},{7,8},{8,9},{9,10},{10,1... | collective-permute-start | bytes 294920 | tf_op jit(solution)/shard_map/ppermute | solution.py:24
  64.9 2.7 copy-start.20
  64.9 4.6 %collective-permute-start.5 = (f32[192,128]{1,0:T(8,128)S(1)}, f32[192,128]{1,0:T(8,128)S(1)}, u32[]{:S(2)}, u32[]{:S(2)}) collective-permute-start(f32[192,128]{1,0:T(8,128)S(1)} %get-tuple-element.73), channel_id=1, source_target_pairs={{1,0},{2,1},{3,2},{4,3},{5,4},{6,5},{7,6},{8,7},{9,8},{10,9},{11,1... | collective-permute-start | bytes 294920 | tf_op jit(solution)/shard_map/ppermute | solution.py:25
  71.0 1.4 copy-start.60
  73.9 1.4 copy-start.23
  78.7 1.4 copy-start.33
  80.1 1.1 copy-start.42
  80.1 1.1 copy-start.85
  85.1 7.6 %collective-permute-start.6 = (f32[192,128]{1,0:T(8,128)S(1)}, f32[192,128]{1,0:T(8,128)S(1)}, u32[]{:S(2)}, u32[]{:S(2)}) collective-permute-start(f32[192,128]{1,0:T(8,128)S(1)} %get-tuple-element.70), channel_id=1, source_target_pairs={{0,1},{1,2},{2,3},{3,4},{4,5},{5,6},{6,7},{7,8},{8,9},{9,10},{10,1... | collective-permute-start | bytes 294920 | tf_op jit(solution)/shard_map/ppermute | solution.py:24
  89.6 4.1 %collective-permute-start.7 = (f32[192,128]{1,0:T(8,128)S(1)}, f32[192,128]{1,0:T(8,128)S(1)}, u32[]{:S(2)}, u32[]{:S(2)}) collective-permute-start(f32[192,128]{1,0:T(8,128)S(1)} %get-tuple-element.71), channel_id=1, source_target_pairs={{1,0},{2,1},{3,2},{4,3},{5,4},{6,5},{7,6},{8,7},{9,8},{10,9},{11,1... | collective-permute-start | bytes 294920 | tf_op jit(solution)/shard_map/ppermute | solution.py:25
  101.4 1.4 copy-start.93
  104.6 0.9 copy-start.70
  104.6 1.4 copy-start.53
  105.5 0.9 copy-start.16
  105.5 1.0 copy-start.19
  105.5 1.1 copy-start.22
  107.8 9.4 %collective-permute-start.8 = (f32[192,128]{1,0:T(8,128)S(1)}, f32[192,128]{1,0:T(8,128)S(1)}, u32[]{:S(2)}, u32[]{:S(2)}) collective-permute-start(f32[192,128]{1,0:T(8,128)S(1)} %get-tuple-element.68), channel_id=1, source_target_pairs={{0,1},{1,2},{2,3},{3,4},{4,5},{5,6},{6,7},{7,8},{8,9},{9,10},{10,1... | collective-permute-start | bytes 294920 | tf_op jit(solution)/shard_map/ppermute | solution.py:24
  113.7 4.1 %collective-permute-start.9 = (f32[192,128]{1,0:T(8,128)S(1)}, f32[192,128]{1,0:T(8,128)S(1)}, u32[]{:S(2)}, u32[]{:S(2)}) collective-permute-start(f32[192,128]{1,0:T(8,128)S(1)} %get-tuple-element.69), channel_id=1, source_target_pairs={{1,0},{2,1},{3,2},{4,3},{5,4},{6,5},{7,6},{8,7},{9,8},{10,9},{11,1... | collective-permute-start | bytes 294920 | tf_op jit(solution)/shard_map/ppermute | solution.py:25
  119.4 1.4 copy-start.62
  122.2 1.4 copy-start.24
  127.1 1.4 copy-start.34
  128.5 1.1 copy-start.44
  128.5 1.1 copy-start.87
  133.5 9.2 %collective-permute-start.10 = (f32[192,128]{1,0:T(8,128)S(1)}, f32[192,128]{1,0:T(8,128)S(1)}, u32[]{:S(2)}, u32[]{:S(2)}) collective-permute-start(f32[192,128]{1,0:T(8,128)S(1)} %get-tuple-element.66), channel_id=1, source_target_pairs={{0,1},{1,2},{2,3},{3,4},{4,5},{5,6},{6,7},{7,8},{8,9},{9,10},{10,1... | collective-permute-start | bytes 294920 | tf_op jit(solution)/shard_map/ppermute | solution.py:24
  139.4 4.1 %collective-permute-start.11 = (f32[192,128]{1,0:T(8,128)S(1)}, f32[192,128]{1,0:T(8,128)S(1)}, u32[]{:S(2)}, u32[]{:S(2)}) collective-permute-start(f32[192,128]{1,0:T(8,128)S(1)} %get-tuple-element.67), channel_id=1, source_target_pairs={{1,0},{2,1},{3,2},{4,3},{5,4},{6,5},{7,6},{8,7},{9,8},{10,9},{11,1... | collective-permute-start | bytes 294920 | tf_op jit(solution)/shard_map/ppermute | solution.py:25
  153.5 1.4 copy-start.51
  154.4 0.9 copy-start.15
  154.4 1.0 copy-start.17
  154.4 1.1 copy-start.21
  157.1 8.0 %copy-start.28 = (f32[64,256]{1,0:T(8,128)S(1)}, f32[64,256]{1,0:T(8,128)}, u32[]{:S(2)}) copy-start(f32[64,256]{1,0:T(8,128)} %reduce_sum.77) | copy-start | bytes 196612
  157.1 8.0 %copy-start.30 = (f32[64,256]{1,0:T(8,128)S(1)}, f32[64,256]{1,0:T(8,128)}, u32[]{:S(2)}) copy-start(f32[64,256]{1,0:T(8,128)} %reduce_sum.78) | copy-start | bytes 196612
  157.1 8.0 %copy-start.32 = (f32[64,256]{1,0:T(8,128)S(1)}, f32[64,256]{1,0:T(8,128)}, u32[]{:S(2)}) copy-start(f32[64,256]{1,0:T(8,128)} %multiply_reduce_fusion) | copy-start | bytes 196612
  157.1 8.6 %collective-permute-start.12 = (f32[192,128]{1,0:T(8,128)S(1)}, f32[192,128]{1,0:T(8,128)S(1)}, u32[]{:S(2)}, u32[]{:S(2)}) collective-permute-start(f32[192,128]{1,0:T(8,128)S(1)} %get-tuple-element.64), channel_id=1, source_target_pairs={{0,1},{1,2},{2,3},{3,4},{4,5},{5,6},{6,7},{7,8},{8,9},{9,10},{10,1... | collective-permute-start | bytes 294920 | tf_op jit(solution)/shard_map/ppermute | solution.py:24
  163.1 4.1 %collective-permute-start.13 = (f32[192,128]{1,0:T(8,128)S(1)}, f32[192,128]{1,0:T(8,128)S(1)}, u32[]{:S(2)}, u32[]{:S(2)}) collective-permute-start(f32[192,128]{1,0:T(8,128)S(1)} %get-tuple-element.65), channel_id=1, source_target_pairs={{1,0},{2,1},{3,2},{4,3},{5,4},{6,5},{7,6},{8,7},{9,8},{10,9},{11,1... | collective-permute-start | bytes 294920 | tf_op jit(solution)/shard_map/ppermute | solution.py:25
  168.8 1.4 copy-start.64
  171.6 1.4 copy-start.25
  176.5 1.4 copy-start.35
  177.8 1.1 copy-start.46
  177.8 1.1 copy-start.89
  181.9 10.4 %copy-start.9 = (f32[192,256]{1,0:T(8,128)}, f32[192,256]{1,0:T(8,128)S(1)}, u32[]{:S(2)}) copy-start(f32[192,256]{1,0:T(8,128)S(1)} %fusion.6) | copy-start | bytes 589828
  182.2 8.3 %collective-permute-start.14 = (f32[192,128]{1,0:T(8,128)S(1)}, f32[192,128]{1,0:T(8,128)S(1)}, u32[]{:S(2)}, u32[]{:S(2)}) collective-permute-start(f32[192,128]{1,0:T(8,128)S(1)} %get-tuple-element.62), channel_id=1, source_target_pairs={{0,1},{1,2},{2,3},{3,4},{4,5},{5,6},{6,7},{7,8},{8,9},{9,10},{10,1... | collective-permute-start | bytes 294920 | tf_op jit(solution)/shard_map/ppermute | solution.py:24
  188.1 4.1 %collective-permute-start.15 = (f32[192,128]{1,0:T(8,128)S(1)}, f32[192,128]{1,0:T(8,128)S(1)}, u32[]{:S(2)}, u32[]{:S(2)}) collective-permute-start(f32[192,128]{1,0:T(8,128)S(1)} %get-tuple-element.63), channel_id=1, source_target_pairs={{1,0},{2,1},{3,2},{4,3},{5,4},{6,5},{7,6},{8,7},{9,8},{10,9},{11,1... | collective-permute-start | bytes 294920 | tf_op jit(solution)/shard_map/ppermute | solution.py:25
  198.1 1.4 copy-start.95
  201.6 0.9 copy-start.13
  (61 other events, 48.0 us)
Sparse Core Ops, SparseCore 0:
  206.6 164.7 all-reduce.2
where the time goes:
time: 387 us; the launch traced here: 380 us
  waiting for transfers between devices  170 us (44%)
  local copies, waits for them, and re-layouts  88 us (23%)
  starting transfers between devices  54.4 us (14%)
  matrix products  38.7 us (10%)
  between operations  17.2 us (4%)
  other arithmetic  11.3 us (3%)
    unnamed x2, waiting for transfers between devices  163 us
    gather x48, local copies, waits for them, and re-layouts, outer_traces(): pieces.append(jnp.take(rows, position, axis=1) * valid[face])  49.8 us
    ppermute x8, starting transfers between devices, padded(): before = lax.ppermute(last, axis, up)  36.8 us
    dot_general x48, matrix products, flux_term(): jnp.dot(face_table, outer_traces(field), preferred_element_type=jnp.float...  28.5 us
    unnamed x233, local copies, waits for them, and re-layouts  23.7 us
    ppermute x8, starting transfers between devices, padded(): after = lax.ppermute(leading, axis, down)  17.6 us
  transfers between devices with their start and end apart: 17, of which 8 were waited for; matrix products, arithmetic and copies ran while one was open for 4% of the time, Pallas kernels for 0%

commit v1 on v0

v1 whole, which is shorter than its diff:
```python
import functools

import jax
import jax.numpy as jnp
import ml_dtypes
import numpy as np
from jax import lax
from jax.experimental import pallas as pl
from jax.experimental.pallas import tpu as pltpu
from jax.sharding import PartitionSpec as P

STEPS = 4
LAYER = 128
TIME_STEP = 0.025
DAMPING = 0.5
GAIN = 6.0 * TIME_STEP
MESH = pl.DeviceIdType.MESH


def operator_table():
    points = np.array([-1.0, -1.0 / np.sqrt(5.0), 1.0 / np.sqrt(5.0), 1.0])
    barycentric = np.array(
        [1.0 / np.prod([points[j] - points[k] for k in range(4) if k != j]) for j in range(4)]
    )
    deriv = np.zeros((4, 4))
    for row in range(4):
        for column in range(4):
            if row != column:
                deriv[row, column] = (
                    barycentric[column] / barycentric[row] / (points[row] - points[column])
                )
        deriv[row, row] = -np.sum(deriv[row])
    identity = np.eye(4)
    along_x = 2.0 * np.kron(np.kron(deriv, identity), identity)
    along_y = 2.0 * np.kron(np.kron(identity, deriv), identity)
    along_z = 2.0 * np.kron(np.kron(identity, identity), deriv)
    curl = np.zeros((192, 192))
    curl[0:64, 64:128] = -along_z
    curl[0:64, 128:192] = along_y
    curl[64:128, 0:64] = along_z
    curl[64:128, 128:192] = -along_x
    curl[128:192, 0:64] = -along_y
    curl[128:192, 64:128] = along_x
    numbers = np.arange(64).reshape(4, 4, 4)
    faces = [
        numbers[0].ravel(),
        numbers[3].ravel(),
        numbers[:, 0].ravel(),
        numbers[:, 3].ravel(),
        numbers[:, :, 0].ravel(),
        numbers[:, :, 3].ravel(),
    ]
    inner = np.zeros((192, 192))
    for face in range(6):
        direction = face // 2
        sign = 1.0 if face % 2 else -1.0
        for component in range(3):
            for other in range(3):
                parity = (component - direction) * (direction - other) * (other - component) / 2.0
                for node in faces[face]:
                    inner[component * 64 + node, other * 64 + node] += sign * parity
    return inner - curl / 6.0


def split_table():
    table = operator_table()
    high = table.astype(ml_dtypes.bfloat16)
    low = (table - high.astype(np.float64)).astype(ml_dtypes.bfloat16)
    return np.concatenate([high, low], axis=0)


def halves(value):
    high = value.astype(jnp.bfloat16)
    low = (value - high.astype(jnp.float32)).astype(jnp.bfloat16)
    return high, low


def pick(value, index):
    index = jnp.broadcast_to(index, value.shape)
    return jnp.take_along_axis(value, index, axis=1, mode="promise_in_bounds")


def rows_of(ref, layer, start):
    return jnp.concatenate(
        [ref[layer, 64 + start : 80 + start], ref[layer, 128 + start : 144 + start]], axis=0
    )


def kernel(
    n_exc,
    n_space,
    adj_e,
    adj_h,
    adj_j,
    fwd_e,
    inv_eps,
    drude,
    neighbor,
    design,
    ports,
    profile,
    table,
    out_e,
    out_h,
    out_eps,
    out_drude,
    e_ref,
    h_ref,
    j_ref,
    s_ref,
    g_ref,
    f_ref,
    v_ref,
    w_ref,
    nb_ref,
    dm_ref,
    pe_ref,
    pp_ref,
    tb_ref,
    send_e,
    send_h,
    recv_e,
    recv_h,
    sums,
    parts,
    load_sem,
    send_sem,
    recv_sem,
    part_send_sem,
    part_recv_sem,
    store_sem,
):
    me_exc = lax.axis_index("exc")
    me_space = lax.axis_index("space")
    left = lax.rem(me_space + n_space - 1, n_space)
    right = lax.rem(me_space + 1, n_space)
    own_rows = LAYER // n_exc

    loads = []

    def load(src, dst):
        copy = pltpu.make_async_copy(src, dst, load_sem.at[len(loads)])
        copy.start()
        loads.append(copy)
        return copy

    def load_layers(src, dst):
        return [load(src.at[..., pl.ds(n * LAYER, LAYER)], dst.at[n]) for n in range(2)]

    got_nb = load(neighbor, nb_ref)
    got_e = load_layers(adj_e.at[0], e_ref)
    got_tb = load(table, tb_ref)
    got_h = load_layers(adj_h.at[0], h_ref)
    got_w = load_layers(drude, w_ref)
    got_v = load_layers(inv_eps, v_ref)
    got_j = load_layers(adj_j.at[0], j_ref)
    got_pe = load(ports, pe_ref)
    got_pp = load(profile.at[0], pp_ref)
    got_f = load_layers(fwd_e.at[0], f_ref)
    got_dm = load(design, dm_ref)

    barrier = pltpu.get_barrier_semaphore()
    for peer in (left, right):
        pl.semaphore_signal(barrier, inc=1, device_id={"space": peer}, device_id_type=MESH)
    for hop in range(1, n_exc):
        peer = lax.rem(me_exc + hop, n_exc)
        pl.semaphore_signal(barrier, inc=1, device_id={"exc": peer}, device_id_type=MESH)

    sublane = lax.broadcasted_iota(jnp.int32, (8, LAYER), 0)
    lower = sublane < 4

    got_nb.wait()
    table_nb = nb_ref[...]
    place = table_nb & (LAYER - 1)

    def face(number, layer):
        return place[number : number + 1, layer * LAYER : (layer + 1) * LAYER]

    def inside(number, layer):
        cut = table_nb[number : number + 1, layer * LAYER : (layer + 1) * LAYER]
        return (cut >= 0).astype(jnp.float32)

    along_y = [jnp.where(lower, face(3, n), face(2, n)) for n in range(2)]
    along_y = [jnp.concatenate([index] * 8, axis=0) for index in along_y]
    low_z = [face(4, n) for n in range(2)]
    high_z = [face(5, n) for n in range(2)]
    between = [face(1, 0), face(0, 1)]
    beyond = [face(0, 0), face(1, 1)]
    exists = [inside(0, 0), inside(1, 1)]

    def fill_local(field_ref):
        field = jnp.concatenate([field_ref[0], field_ref[1]], axis=1)
        high, low = halves(field)
        whole = jnp.dot(tb_ref[...], high, preferred_element_type=jnp.float32)
        rest = jnp.dot(tb_ref[0:192, :], low, preferred_element_type=jnp.float32)
        total = whole[0:192] + (whole[192:384] + rest)
        zeros = jnp.zeros((48, LAYER), jnp.float32)
        for n in range(2):
            own = field_ref[n].reshape(3, 4, 2, 8, LAYER)
            edge = jnp.concatenate(
                [
                    jnp.where(lower, own[0, :, 0], own[0, :, 1]),
                    jnp.where(lower, own[2, :, 0], own[2, :, 1]),
                ],
                axis=0,
            )
            outer = pick(edge.reshape(64, LAYER), along_y[n]).reshape(8, 8, LAYER)
            outer = pltpu.roll(outer, 4, 1)
            zero = jnp.zeros((4, 8, LAYER), jnp.float32)
            o_x, o_z = outer[0:4], outer[4:8]
            to_x = jnp.stack([jnp.where(lower, o_z, zero), jnp.where(lower, zero, -o_z)], axis=1)
            to_z = jnp.stack([jnp.where(lower, -o_x, zero), jnp.where(lower, zero, o_x)], axis=1)
            if n == 0:
                side = pick(rows_of(field_ref, 1, 0), between[0])
                to_y = jnp.concatenate([zeros, side[16:32]], axis=0)
                to_z2 = jnp.concatenate([zeros, -side[0:16]], axis=0)
            else:
                side = pick(rows_of(field_ref, 0, 48), between[1])
                to_y = jnp.concatenate([-side[16:32], zeros], axis=0)
                to_z2 = jnp.concatenate([side[0:16], zeros], axis=0)
            mine = total[:, n * LAYER : (n + 1) * LAYER]
            g_ref[n, 0:64] = mine[0:64] + to_x.reshape(64, LAYER)
            g_ref[n, 64:128] = mine[64:128] + to_y
            g_ref[n, 128:192] = mine[128:192] + to_z.reshape(64, LAYER) + to_z2
            far = pick(field_ref[n, pl.ds(0, 32, stride=4), :], high_z[n])
            g_ref[n, pl.ds(3, 32, stride=4), :] += jnp.concatenate(
                [far[16:32], -far[0:16]], axis=0
            )
            near = pick(field_ref[n, pl.ds(3, 32, stride=4), :], low_z[n])
            g_ref[n, pl.ds(0, 32, stride=4), :] += jnp.concatenate(
                [-near[16:32], near[0:16]], axis=0
            )

    def exchange(step, kind, src, dst):
        copies = []
        for side, peer in ((0, left), (1, right)):
            copy = pltpu.make_async_remote_copy(
                src_ref=src.at[step, side],
                dst_ref=dst.at[step, 1 - side],
                send_sem=send_sem.at[step, kind, side],
                recv_sem=recv_sem.at[step, kind, 1 - side],
                device_id={"space": peer},
                device_id_type=MESH,
            )
            copy.start()
            copies.append(copy)
        return copies

    sens = [[jnp.zeros((64, LAYER), jnp.float32)] * 2 for _ in range(2)]

    def add_eps(step):
        for n in range(2):
            change = f_ref[n, step + 1].astype(jnp.float32) - f_ref[n, step].astype(jnp.float32)
            product = (e_ref[n] * change).reshape(3, 64, LAYER)
            sens[0][n] = sens[0][n] + (product[0] + product[1] + product[2])

    for copy in got_e:
        copy.wait()

    for step in range(STEPS):
        send_e[step, 0] = rows_of(e_ref, 0, 0)
        send_e[step, 1] = rows_of(e_ref, 1, 48)
        if step == 0:
            pl.semaphore_wait(barrier, 2 + n_exc - 1)
        e_copies = exchange(step, 0, send_e, recv_e)

        if step == 0:
            got_tb.wait()
        fill_local(e_ref)
        if step == 0:
            for copy in got_h:
                copy.wait()
        for n in range(2):
            h_ref[n] = h_ref[n] + GAIN * g_ref[n]
        send_h[step, 0] = rows_of(h_ref, 0, 0)
        send_h[step, 1] = rows_of(h_ref, 1, 48)
        h_copies = exchange(step, 1, send_h, recv_h)

        if step == 0:
            for copy in got_w + got_v + got_j + [got_pe, got_pp]:
                copy.wait()
            element = lax.broadcasted_iota(jnp.int32, (2 * LAYER, LAYER), 0)
            chosen = ((pe_ref[...] & (2 * LAYER - 1)) == element).astype(jnp.bfloat16)
            high, low = halves(pp_ref[...])
            contract = (((1,), (1,)), ((), ()))
            source = lax.dot_general(
                high, chosen, contract, preferred_element_type=jnp.float32
            ) + lax.dot_general(low, chosen, contract, preferred_element_type=jnp.float32)
            for n in range(2):
                s_ref[n] = source[:, n * LAYER : (n + 1) * LAYER]
            for copy in got_f:
                copy.wait()
        else:
            add_eps(step - 1)
        for n in range(2):
            current = j_ref[n].reshape(3, 64, LAYER)
            electric = e_ref[n].reshape(3, 64, LAYER)
            current = (1.0 - TIME_STEP * DAMPING) * current + (TIME_STEP * w_ref[n]) * electric
            j_ref[n] = current.reshape(192, LAYER)
            before = f_ref[n, step].astype(jnp.float32).reshape(3, 64, LAYER)
            product = current * before
            sens[1][n] = sens[1][n] + (product[0] + product[1] + product[2])
            drive = (TIME_STEP * v_ref[n]) * (current + s_ref[n].reshape(3, 64, LAYER))
            e_ref[n] = (electric - drive).reshape(192, LAYER)

        for copy in e_copies:
            copy.wait_recv()
        outer = pick(recv_e[step, 0], beyond[0]) * (GAIN * exists[0])
        h_ref[0, 64:80] += -outer[16:32]
        h_ref[0, 128:144] += outer[0:16]
        outer = pick(recv_e[step, 1], beyond[1]) * (GAIN * exists[1])
        h_ref[1, 112:128] += outer[16:32]
        h_ref[1, 176:192] += -outer[0:16]

        fill_local(h_ref)
        if step == STEPS - 1:
            stores = [
                pltpu.make_async_copy(
                    h_ref.at[n], out_h.at[0, :, pl.ds(n * LAYER, LAYER)], store_sem.at[n]
                )
                for n in range(2)
            ]
            for copy in stores:
                copy.start()

        for n in range(2):
            kick = (GAIN * v_ref[n]) * g_ref[n].reshape(3, 64, LAYER)
            e_ref[n] = e_ref[n] - kick.reshape(192, LAYER)
        for copy in h_copies:
            copy.wait_recv()
        outer = pick(recv_h[step, 0], beyond[0])
        own = GAIN * send_e[step, 0]
        speed = (GAIN * v_ref[0, 0:16]) * exists[0]
        e_ref[0, 64:80] += speed * (outer[16:32] - own[0:16])
        e_ref[0, 128:144] += -speed * (outer[0:16] + own[16:32])
        outer = pick(recv_h[step, 1], beyond[1])
        own = GAIN * send_e[step, 1]
        speed = (GAIN * v_ref[1, 48:64]) * exists[1]
        e_ref[1, 112:128] += -speed * (outer[16:32] + own[0:16])
        e_ref[1, 176:192] += speed * (outer[0:16] - own[16:32])
        for copy in e_copies + h_copies:
            copy.wait_send()

    for n in range(2):
        copy = pltpu.make_async_copy(
            e_ref.at[n], out_e.at[0, :, pl.ds(n * LAYER, LAYER)], store_sem.at[2 + n]
        )
        copy.start()
        stores.append(copy)
    add_eps(STEPS - 1)
    got_dm.wait()
    pixel = lax.broadcasted_iota(jnp.int32, (LAYER, 2 * LAYER), 0)
    members = ((dm_ref[...] & (LAYER - 1)) == pixel).astype(jnp.bfloat16)
    stacked = jnp.concatenate(
        [jnp.concatenate(sens[0], axis=1), jnp.concatenate(sens[1], axis=1)], axis=0
    )
    high, low = halves(stacked)
    contract = (((1,), (1,)), ((), ()))
    sums[...] = lax.dot_general(
        members, high, contract, preferred_element_type=jnp.float32
    ) + lax.dot_general(members, low, contract, preferred_element_type=jnp.float32)
    part_copies = []
    for hop in range(1, n_exc):
        peer = lax.rem(me_exc + hop, n_exc)
        start = pl.multiple_of(peer * own_rows, own_rows)
        copy = pltpu.make_async_remote_copy(
            src_ref=sums.at[pl.ds(start, own_rows)],
            dst_ref=parts.at[hop],
            send_sem=part_send_sem.at[hop],
            recv_sem=part_recv_sem.at[hop],
            device_id={"exc": peer},
            device_id_type=MESH,
        )
        copy.start()
        part_copies.append(copy)
    total = sums[pl.ds(pl.multiple_of(me_exc * own_rows, own_rows), own_rows)]
    for hop in range(1, n_exc):
        part_copies[hop - 1].wait_recv()
        total = total + parts[hop]
    total = total * (1.0 / n_exc)
    out_eps[...] = total[:, 0:64]
    out_drude[...] = total[:, 64:128]
    for copy in part_copies:
        copy.wait_send()
    for copy in stores:
        copy.wait()


def local(n_exc, n_space, *args):
    (adj_e, adj_h, adj_j, fwd_e, inv_eps, drude, neighbor, design, ports, profile) = args
    own_rows = LAYER // n_exc
    f32 = jnp.float32
    anywhere = pl.BlockSpec(memory_space=pltpu.HBM)
    in_vmem = pl.BlockSpec(memory_space=pltpu.VMEM)
    new_e, new_h, grad_eps, grad_drude = pl.pallas_call(
        functools.partial(kernel, n_exc, n_space),
        out_shape=(
            jax.ShapeDtypeStruct(adj_e.shape, f32),
            jax.ShapeDtypeStruct(adj_h.shape, f32),
            jax.ShapeDtypeStruct((own_rows, 64), f32),
            jax.ShapeDtypeStruct((own_rows, 64), f32),
        ),
        in_specs=[anywhere] * 11,
        out_specs=(anywhere, anywhere, in_vmem, in_vmem),
        scratch_shapes=[
            pltpu.VMEM((2, 192, LAYER), f32),
            pltpu.VMEM((2, 192, LAYER), f32),
            pltpu.VMEM((2, 192, LAYER), f32),
            pltpu.VMEM((2, 192, LAYER), f32),
            pltpu.VMEM((2, 192, LAYER), f32),
            pltpu.VMEM((2, STEPS + 1, 192, LAYER), jnp.bfloat16),
            pltpu.VMEM((2, 64, LAYER), f32),
            pltpu.VMEM((2, 64, LAYER), f32),
            pltpu.VMEM((6, 2 * LAYER), jnp.int32),
            pltpu.VMEM((1, 2 * LAYER), jnp.int32),
            pltpu.VMEM((1, LAYER), jnp.int32),
            pltpu.VMEM((192, LAYER), f32),
            pltpu.VMEM((384, 192), jnp.bfloat16),
            pltpu.VMEM((STEPS, 2, 32, LAYER), f32),
            pltpu.VMEM((STEPS, 2, 32, LAYER), f32),
            pltpu.VMEM((STEPS, 2, 32, LAYER), f32),
            pltpu.VMEM((STEPS, 2, 32, LAYER), f32),
            pltpu.VMEM((LAYER, LAYER), f32),
            pltpu.VMEM((n_exc, own_rows, LAYER), f32),
            pltpu.SemaphoreType.DMA((20,)),
            pltpu.SemaphoreType.DMA((STEPS, 2, 2)),
            pltpu.SemaphoreType.DMA((STEPS, 2, 2)),
            pltpu.SemaphoreType.DMA((n_exc,)),
            pltpu.SemaphoreType.DMA((n_exc,)),
            pltpu.SemaphoreType.DMA((4,)),
        ],
        compiler_params=pltpu.CompilerParams(
            collective_id=0, has_side_effects=True, vmem_limit_bytes=60 << 20
        ),
        name="adjoint_steps",
    )(
        adj_e,
        adj_h,
        adj_j,
        fwd_e,
        inv_eps,
        drude,
        neighbor,
        design.reshape(1, 2 * LAYER),
        ports,
        profile,
        jnp.asarray(split_table()),
    )
    return new_e, new_h, grad_eps.T, grad_drude.T


def solution(mesh):
    return jax.shard_map(
        functools.partial(local, mesh.shape["exc"], mesh.shape["space"]),
        mesh=mesh,
        in_specs=(
            P("exc", None, "space"),
            P("exc", None, "space"),
            P("exc", None, "space"),
            P("exc", None, None, "space"),
            P(None, "space"),
            P(None, "space"),
            P(None, "space"),
            P("space"),
            P("exc", "space"),
            P("exc", None, "space"),
        ),
        out_specs=(
            P("exc", None, "space"),
            P("exc", None, "space"),
            P(None, ("space", "exc")),
            P(None, ("space", "exc")),
        ),
        check_vma=False,
    )
```

time: 387 us -> 34.9 us (0.09)
  the two profiles are of different devices: /device:TPU:2 before, /device:TPU:32 now
where the time goes in v1:
time: 34.9 us; the launch traced here: 34.7 us
  Pallas kernels  30.4 us (87%)
  local copies, waits for them, and re-layouts  3.61 us (10%)
  between operations  0.65 us (2%)
    pallas_call x1, Pallas kernels, local(): pl.pallas_call(functools.partial(kernel, n_exc, n_space), out_shape=(jax....  30.4 us
    unnamed x10, local copies, waits for them, and re-layouts  3.61 us

profile of v1, /device:TPU:32, one launch (start us, length us, event | category | flops | bytes accessed | tf_op | source)
XLA Modules:
  0.0 34.7 jit_solution(1816485577530421076)
XLA Ops:
  0.6 30.4 %adjoint_steps.1 = (f32[1,192,256]{2,1,0:T(8,128)}, f32[1,192,256]{2,1,0:T(8,128)}, f32[8,64]{1,0:T(8,128)}, f32[8,64]{1,0:T(8,128)}) custom-call(f32[1,192,256]{2,1,0:T(8,128)} %adj_e.1, f32[1,192,256]{2,1,0:T(8,128)} %adj_h.1, f32[1,192,256]{2,1,0:T(8,128)} %adj_j.1, bf16[1,5,192,256]{3,2,1,0:T(8,128)(2,1)} %fwd_e.1, f32[64,256]{1,0:T(8,128)} %inv_eps.1, ...), custom_call_target="tpu_custom_call" | custom-call | tf_op jit(solution)/shard_map/adjoint_steps/pallas_call | solution.py:395
  31.1 0.0 copy-start
  31.1 1.7 %copy.19 = f32[1,192,256]{2,1,0:T(8,128)} copy(f32[1,192,256]{2,1,0:T(8,128)} %get-tuple-element.16) | data formatting | bytes 393216
  32.7 0.0 copy-done
  32.7 0.0 copy-start.2
  32.7 0.7 %copy.20 = f32[1,192,256]{2,1,0:T(8,128)} copy(f32[1,192,256]{2,1,0:T(8,128)S(1)} %copy-done) | data formatting | bytes 393216
  33.4 0.0 copy-done.2
  33.4 0.0 copy-start.1
  33.4 0.6 %copy.21 = f32[64,8]{0,1:T(8,128)} copy(f32[64,8]{0,1:T(8,128)S(1)} %bitcast.4) | data formatting | bytes 4096
  34.0 0.1 copy-done.1
  34.1 0.6 %copy.22 = f32[64,8]{0,1:T(8,128)} copy(f32[64,8]{0,1:T(8,128)S(1)} %bitcast.3) | data formatting | bytes 4096
Async XLA Ops:
  31.1 1.7 %copy-start = (f32[1,192,256]{2,1,0:T(8,128)S(1)}, f32[1,192,256]{2,1,0:T(8,128)}, u32[]{:S(2)}) copy-start(f32[1,192,256]{2,1,0:T(8,128)} %get-tuple-element.17) | copy-start | bytes 589828
  32.7 0.7 %copy-start.2 = (f32[8,64]{1,0:T(8,128)S(1)}, f32[8,64]{1,0:T(8,128)}, u32[]{:S(2)}) copy-start(f32[8,64]{1,0:T(8,128)} %get-tuple-element.10) | copy-start | bytes 6148
  33.4 0.7 %copy-start.1 = (f32[8,64]{1,0:T(8,128)S(1)}, f32[8,64]{1,0:T(8,128)}, u32[]{:S(2)}) copy-start(f32[8,64]{1,0:T(8,128)} %get-tuple-element.11) | copy-start | bytes 6148

commit v2 on v1

--- a/solution.py
+++ b/solution.py
@@ -386,6 +386,32 @@
         copy.wait()
 
 
+def write_kernel(e_in, h_in, a_in, b_in, e_out, h_out, a_out, b_out, sem):
+    copies = [
+        pltpu.make_async_copy(src, dst, sem.at[at])
+        for at, (src, dst) in enumerate(
+            ((e_in, e_out), (h_in, h_out), (a_in, a_out), (b_in, b_out))
+        )
+    ]
+    for copy in copies:
+        copy.start()
+    for copy in copies:
+        copy.wait()
+
+
+def write(*arrays):
+    spec = pl.BlockSpec(memory_space=pltpu.HBM)
+    return pl.pallas_call(
+        write_kernel,
+        out_shape=tuple(jax.ShapeDtypeStruct(a.shape, a.dtype) for a in arrays),
+        in_specs=[pl.BlockSpec(memory_space=pltpu.VMEM)] * 4,
+        out_specs=(spec,) * 4,
+        scratch_shapes=[pltpu.SemaphoreType.DMA((4,))],
+        compiler_params=pltpu.CompilerParams(vmem_limit_bytes=2 << 20),
+        name="write_out",
+    )(*arrays)
+
+
 def local(n_exc, n_space, *args):
     (adj_e, adj_h, adj_j, fwd_e, inv_eps, drude, neighbor, design, ports, profile) = args
     own_rows = LAYER // n_exc
@@ -430,22 +456,13 @@
             pltpu.SemaphoreType.DMA((4,)),
         ],
         compiler_params=pltpu.CompilerParams(
-            collective_id=0, has_side_effects=True, vmem_limit_bytes=60 << 20
+            collective_id=0, has_side_effects=True, vmem_limit_bytes=16 << 20
         ),
         name="adjoint_steps",
     )(
-        adj_e,
-        adj_h,
-        adj_j,
-        fwd_e,
-        inv_eps,
-        drude,
-        neighbor,
-        design.reshape(1, 2 * LAYER),
-        ports,
-        profile,
-        jnp.asarray(split_table()),
+        *[pltpu.with_memory_space_constraint(x, pltpu.HBM) for x in (adj_e, adj_h, adj_j, fwd_e, inv_eps, drude, neighbor, design.reshape(1, 2 * LAYER), ports, profile, jnp.asarray(split_table()))]
     )
+    new_e, new_h, grad_eps, grad_drude = write(new_e, new_h, grad_eps, grad_drude)
     return new_e, new_h, grad_eps.T, grad_drude.T
 
 

time: 34.9 us -> 31.5 us (0.903)
  local copies, waits for them, and re-layouts: 3.61 us -> 0 us
    unnamed x10 -> x0, local copies, waits for them, and re-layouts: 3.61 us -> none
    pallas_call x0 -> x1, Pallas kernels: none -> 0.78 us  [write(): pl.pallas_call(write_kernel, out_shape=tuple((jax.ShapeDtypeStruct(a.shap...]
    pallas_call x1, Pallas kernels: 30.4 us -> 29.9 us  [local(): pl.pallas_call(functools.partial(kernel, n_exc, n_space), out_shape=(jax....]
where the time goes in v2:
time: 31.5 us; the launch traced here: 31.3 us
  Pallas kernels  30.7 us (97%)
  between operations  0.64 us (2%)
    pallas_call x1, Pallas kernels, local(): pl.pallas_call(functools.partial(kernel, n_exc, n_space), out_shape=(jax....  29.9 us
    pallas_call x1, Pallas kernels, write(): pl.pallas_call(write_kernel, out_shape=tuple((jax.ShapeDtypeStruct(a.shap...  0.78 us

profile of v2, /device:TPU:32, one launch (start us, length us, event | category | flops | bytes accessed | tf_op | source)
XLA Modules:
  0.0 31.3 jit_solution(17500230354611695872)
XLA Ops:
  0.6 29.9 %adjoint_steps.1 = (f32[1,192,256]{2,1,0:T(8,128)S(1)}, f32[1,192,256]{2,1,0:T(8,128)S(1)}, f32[8,64]{1,0:T(8,128)S(1)}, f32[8,64]{1,0:T(8,128)S(1)}) custom-call(f32[1,192,256]{2,1,0:T(8,128)} %adj_e.1, f32[1,192,256]{2,1,0:T(8,128)} %adj_h.1, f32[1,192,256]{2,1,0:T(8,128)} %adj_j.1, bf16[1,5,192,256]{3,2,1,0:T(8,128)(2,1)} %fwd_e.1, f32[64,256]{1,0:T(8,128)} %inv_eps.1, ...), custom_call_target="tpu_custom_call" | custom-call | tf_op jit(solution)/shard_map/adjoint_steps/pallas_call | solution.py:421
  30.5 0.8 %write_out.1 = (f32[1,192,256]{2,1,0:T(8,128)}, f32[1,192,256]{2,1,0:T(8,128)}, f32[8,64]{1,0:T(8,128)}, f32[8,64]{1,0:T(8,128)}) custom-call(f32[1,192,256]{2,1,0:T(8,128)S(1)} %get-tuple-element.12.e_in, f32[1,192,256]{2,1,0:T(8,128)S(1)} %get-tuple-element.13.h_in, f32[8,64]{1,0:T(8,128)S(1)} %get-tuple-element.14.a_in, f32[8,64]{1,0:T(8,128)S(1)} %get-tuple-element.15.b_in), custom_call_target="tpu_custom_call" | custom-call | tf_op jit(solution)/shard_map/write_out/pallas_call | solution.py:404

commit v3 on v2

v3 whole, which is shorter than its diff:
```python
import functools

import jax
import jax.numpy as jnp
import ml_dtypes
import numpy as np
from jax import lax
from jax.experimental import pallas as pl
from jax.experimental.pallas import tpu as pltpu
from jax.sharding import PartitionSpec as P

STEPS = 4
LAYER = 128
TIME_STEP = 0.025
DAMPING = 0.5
GAIN = 6.0 * TIME_STEP
MESH = pl.DeviceIdType.MESH


def operator_table():
    points = np.array([-1.0, -1.0 / np.sqrt(5.0), 1.0 / np.sqrt(5.0), 1.0])
    barycentric = np.array(
        [1.0 / np.prod([points[j] - points[k] for k in range(4) if k != j]) for j in range(4)]
    )
    deriv = np.zeros((4, 4))
    for row in range(4):
        for column in range(4):
            if row != column:
                deriv[row, column] = (
                    barycentric[column] / barycentric[row] / (points[row] - points[column])
                )
        deriv[row, row] = -np.sum(deriv[row])
    identity = np.eye(4)
    along_x = 2.0 * np.kron(np.kron(deriv, identity), identity)
    along_y = 2.0 * np.kron(np.kron(identity, deriv), identity)
    along_z = 2.0 * np.kron(np.kron(identity, identity), deriv)
    curl = np.zeros((192, 192))
    curl[0:64, 64:128] = -along_z
    curl[0:64, 128:192] = along_y
    curl[64:128, 0:64] = along_z
    curl[64:128, 128:192] = -along_x
    curl[128:192, 0:64] = -along_y
    curl[128:192, 64:128] = along_x
    numbers = np.arange(64).reshape(4, 4, 4)
    faces = [
        numbers[0].ravel(),
        numbers[3].ravel(),
        numbers[:, 0].ravel(),
        numbers[:, 3].ravel(),
        numbers[:, :, 0].ravel(),
        numbers[:, :, 3].ravel(),
    ]
    inner = np.zeros((192, 192))
    for face in range(6):
        direction = face // 2
        sign = 1.0 if face % 2 else -1.0
        for component in range(3):
            for other in range(3):
                parity = (component - direction) * (direction - other) * (other - component) / 2.0
                for node in faces[face]:
                    inner[component * 64 + node, other * 64 + node] += sign * parity
    return inner - curl / 6.0


def split_table():
    table = operator_table()
    high = table.astype(ml_dtypes.bfloat16)
    low = (table - high.astype(np.float64)).astype(ml_dtypes.bfloat16)
    return np.concatenate([high, low], axis=0)


def split_faces():
    table = split_table()
    tables = []
    for start in (0, 48):
        rows = np.concatenate([np.arange(64, 80), np.arange(128, 144)]) + start
        high, low = table[0:192, rows], table[192:384, rows]
        tables.append(np.concatenate([high, low, high], axis=1))
    return np.stack(tables)


def halves(value):
    high = value.astype(jnp.bfloat16)
    low = (value - high.astype(jnp.float32)).astype(jnp.bfloat16)
    return high, low


def pick(value, index):
    index = jnp.broadcast_to(index, value.shape)
    return jnp.take_along_axis(value, index, axis=1, mode="promise_in_bounds")


def rows_of(ref, layer, start):
    return jnp.concatenate(
        [ref[layer, 64 + start : 80 + start], ref[layer, 128 + start : 144 + start]], axis=0
    )


def turn(trace, sign):
    return jnp.concatenate([sign * trace[16:32], -sign * trace[0:16]], axis=0)


def add_rows(ref, layer, start, value):
    ref[layer, 64 + start : 80 + start] += value[0:16]
    ref[layer, 128 + start : 144 + start] += value[16:32]


MINE = (0, 48)
THEIRS = (48, 0)
SIGN = (-1.0, 1.0)


def kernel(
    n_exc,
    n_space,
    adj_e,
    adj_h,
    adj_j,
    fwd_e,
    inv_eps,
    drude,
    neighbor,
    design,
    ports,
    profile,
    table,
    face_table,
    out_e,
    out_h,
    out_eps,
    out_drude,
    e_ref,
    h_ref,
    j_ref,
    s_ref,
    g_ref,
    de_ref,
    f_ref,
    v_ref,
    w_ref,
    kick_ref,
    nb_ref,
    dm_ref,
    pe_ref,
    pp_ref,
    tb_ref,
    fb_ref,
    send_t,
    recv_t,
    recv_v,
    recv_nb,
    sums,
    parts,
    load_sem,
    send_sem,
    recv_sem,
    once_send_sem,
    once_recv_sem,
    part_send_sem,
    part_recv_sem,
    store_sem,
):
    me_exc = lax.axis_index("exc")
    me_space = lax.axis_index("space")
    left = lax.rem(me_space + n_space - 1, n_space)
    right = lax.rem(me_space + 1, n_space)
    own_rows = LAYER // n_exc
    f32 = jnp.float32

    barrier = pltpu.get_barrier_semaphore()
    for peer in (left, right):
        pl.semaphore_signal(barrier, inc=1, device_id={"space": peer}, device_id_type=MESH)
    for hop in range(1, n_exc):
        peer = lax.rem(me_exc + hop, n_exc)
        pl.semaphore_signal(barrier, inc=1, device_id={"exc": peer}, device_id_type=MESH)

    loads = []

    def load(src, dst):
        copy = pltpu.make_async_copy(src, dst, load_sem.at[len(loads)])
        copy.start()
        loads.append(copy)
        return copy

    def load_layers(src, dst):
        return [load(src.at[..., pl.ds(n * LAYER, LAYER)], dst.at[n]) for n in range(2)]

    got_nb = load(neighbor, nb_ref)
    got_e = load_layers(adj_e.at[0], e_ref)
    got_tb = load(table, tb_ref)
    got_h = load_layers(adj_h.at[0], h_ref)
    got_v = load_layers(inv_eps, v_ref)
    got_w = load_layers(drude, w_ref)
    got_j = load_layers(adj_j.at[0], j_ref)
    got_pe = load(ports, pe_ref)
    got_pp = load(profile.at[0], pp_ref)
    got_fb = load(face_table, fb_ref)
    got_f = load_layers(fwd_e.at[0], f_ref)
    got_dm = load(design, dm_ref)

    sublane = lax.broadcasted_iota(jnp.int32, (8, LAYER), 0)
    lower = sublane < 4
    first_k = (sublane & 3) == 0
    last_k = (sublane & 3) == 3

    got_nb.wait()
    table_nb = nb_ref[...]
    place = table_nb & (LAYER - 1)

    def face(number, layer):
        return place[number : number + 1, layer * LAYER : (layer + 1) * LAYER]

    def inside(number, layer):
        cut = table_nb[number : number + 1, layer * LAYER : (layer + 1) * LAYER]
        return (cut >= 0).astype(f32)

    edge_y = [jnp.where(lower, face(3, n), face(2, n)) for n in range(2)]
    edge_z = [jnp.where(first_k, face(5, n), face(4, n)) for n in range(2)]
    along_y = [jnp.concatenate([index] * 8, axis=0) for index in edge_y]
    low_z = [face(4, n) for n in range(2)]
    high_z = [face(5, n) for n in range(2)]
    between = [face(1, 0), face(0, 1)]
    beyond = [face(0, 0), face(1, 1)]
    exists = [inside(0, 0), inside(1, 1)]

    def product(field):
        high, low = halves(field)
        whole = jnp.dot(tb_ref[...], high, preferred_element_type=f32)
        rest = jnp.dot(tb_ref[0:192, :], low, preferred_element_type=f32)
        return whole[0:192] + (whole[192:384] + rest)

    def fill_local(field_ref):
        total = product(jnp.concatenate([field_ref[0], field_ref[1]], axis=1))
        zeros = jnp.zeros((48, LAYER), f32)
        for n in range(2):
            own = field_ref[n].reshape(3, 4, 2, 8, LAYER)
            edge = jnp.concatenate(
                [
                    jnp.where(lower, own[0, :, 0], own[0, :, 1]),
                    jnp.where(lower, own[2, :, 0], own[2, :, 1]),
                ],
                axis=0,
            )
            outer = pick(edge.reshape(64, LAYER), along_y[n]).reshape(8, 8, LAYER)
            outer = pltpu.roll(outer, 4, 1)
            zero = jnp.zeros((4, 8, LAYER), f32)
            o_x, o_z = outer[0:4], outer[4:8]
            to_x = jnp.stack([jnp.where(lower, o_z, zero), jnp.where(lower, zero, -o_z)], axis=1)
            to_z = jnp.stack([jnp.where(lower, -o_x, zero), jnp.where(lower, zero, o_x)], axis=1)
            if n == 0:
                side = turn(pick(rows_of(field_ref, 1, 0), between[0]), 1.0)
                to_y = jnp.concatenate([zeros, side[0:16]], axis=0)
                to_z2 = jnp.concatenate([zeros, side[16:32]], axis=0)
            else:
                side = turn(pick(rows_of(field_ref, 0, 48), between[1]), -1.0)
                to_y = jnp.concatenate([side[0:16], zeros], axis=0)
                to_z2 = jnp.concatenate([side[16:32], zeros], axis=0)
            mine = total[:, n * LAYER : (n + 1) * LAYER]
            g_ref[n, 0:64] = mine[0:64] + to_x.reshape(64, LAYER)
            g_ref[n, 64:128] = mine[64:128] + to_y
            g_ref[n, 128:192] = mine[128:192] + to_z.reshape(64, LAYER) + to_z2
            far = pick(field_ref[n, pl.ds(0, 32, stride=4), :], high_z[n])
            g_ref[n, pl.ds(3, 32, stride=4), :] += jnp.concatenate(
                [far[16:32], -far[0:16]], axis=0
            )
            near = pick(field_ref[n, pl.ds(3, 32, stride=4), :], low_z[n])
            g_ref[n, pl.ds(0, 32, stride=4), :] += jnp.concatenate(
                [-near[16:32], near[0:16]], axis=0
            )

    def from_y(rows, index):
        outer = pltpu.roll(pick(jnp.where(lower, rows[0:8], rows[8:16]), index), 4, 0)
        zero = jnp.zeros((8, LAYER), f32)
        return jnp.concatenate(
            [jnp.where(lower, outer, zero), jnp.where(lower, zero, -outer)], axis=0
        )

    def from_z(rows, index):
        parts_z = []
        zero = jnp.zeros((8, LAYER), f32)
        for half in (rows[0:8], rows[8:16]):
            outer = pick(half, index)
            parts_z.append(
                jnp.where(last_k, pltpu.roll(outer, 3, 0), zero)
                - jnp.where(first_k, pltpu.roll(outer, 5, 0), zero)
            )
        return jnp.concatenate(parts_z, axis=0)

    def remote(src, dst, sems, side):
        copy = pltpu.make_async_remote_copy(
            src_ref=src,
            dst_ref=dst,
            send_sem=sems[0],
            recv_sem=sems[1],
            device_id={"space": (left, right)[side]},
            device_id_type=MESH,
        )
        copy.start()
        return copy

    sent = []

    def send_trace(window, kind, ref):
        copies = []
        for side in range(2):
            send_t[window, kind, side] = rows_of(ref, side, MINE[side])
            copies.append(
                remote(
                    send_t.at[window, kind, side],
                    recv_t.at[window, kind, 1 - side],
                    (send_sem.at[window, kind, side], recv_sem.at[window, kind, 1 - side]),
                    side,
                )
            )
        sent.extend(copies)
        return copies

    sens = [[jnp.zeros((64, LAYER), f32)] * 2 for _ in range(2)]

    def add_eps(step):
        for n in range(2):
            change = f_ref[n, step + 1].astype(f32) - f_ref[n, step].astype(f32)
            term = (e_ref[n] * change).reshape(3, 64, LAYER)
            sens[0][n] = sens[0][n] + (term[0] + term[1] + term[2])

    def drive(step):
        for n in range(2):
            electric = e_ref[n].reshape(3, 64, LAYER)
            current = (1.0 - TIME_STEP * DAMPING) * j_ref[n].reshape(3, 64, LAYER)
            current = current + (TIME_STEP * w_ref[n]) * electric
            j_ref[n] = current.reshape(192, LAYER)
            term = current * f_ref[n, step].astype(f32).reshape(3, 64, LAYER)
            sens[1][n] = sens[1][n] + (term[0] + term[1] + term[2])
            push = (TIME_STEP * v_ref[n]) * (current + s_ref[n].reshape(3, 64, LAYER))
            e_ref[n] = (electric - push).reshape(192, LAYER)

    def kick(n):
        return (kick_ref[n] * g_ref[n].reshape(3, 64, LAYER)).reshape(192, LAYER)

    pl.semaphore_wait(barrier, 2 + n_exc - 1)
    once = []
    for side in range(2):
        lanes = pl.ds(side * LAYER, LAYER)
        for at, (src, dst) in enumerate(((inv_eps, recv_v), (neighbor, recv_nb))):
            once.append(
                remote(
                    src.at[:, lanes],
                    dst.at[1 - side],
                    (once_send_sem.at[at, side], once_recv_sem.at[at, 1 - side]),
                    side,
                )
            )
    ghost_y, ghost_z = [None, None], [None, None]

    for copy in got_e:
        copy.wait()

    for window in range(STEPS // 2):
        step = 2 * window
        e0 = send_trace(window, 0, e_ref)
        if window == 0:
            got_tb.wait()
        fill_local(e_ref)
        if window == 0:
            for copy in got_h:
                copy.wait()
        for n in range(2):
            h_ref[n] = h_ref[n] + GAIN * g_ref[n]
        h1 = send_trace(window, 1, h_ref)

        if window == 0:
            for copy in got_w + got_v + got_j + got_f + [got_pe, got_pp, got_fb]:
                copy.wait()
            element = lax.broadcasted_iota(jnp.int32, (2 * LAYER, LAYER), 0)
            chosen = ((pe_ref[...] & (2 * LAYER - 1)) == element).astype(jnp.bfloat16)
            high, low = halves(pp_ref[...])
            contract = (((1,), (1,)), ((), ()))
            source = lax.dot_general(
                high, chosen, contract, preferred_element_type=f32
            ) + lax.dot_general(low, chosen, contract, preferred_element_type=f32)
            for n in range(2):
                s_ref[n] = source[:, n * LAYER : (n + 1) * LAYER]
                kick_ref[n] = GAIN * v_ref[n]
        drive(step)
        fill_local(h_ref)
        for n in range(2):
            e_ref[n] = e_ref[n] - kick(n)
        e1 = send_trace(window, 2, e_ref)
        fill_local(e_ref)
        for n in range(2):
            h_ref[n] = h_ref[n] + GAIN * g_ref[n]
        h2 = send_trace(window, 3, h_ref)

        if window == 0:
            for copy in once:
                copy.wait_recv()
            for side in range(2):
                kick_ref[2 + side] = GAIN * pick(recv_v[side], beyond[side])
                far = recv_nb[side] & (LAYER - 1)
                back = jnp.broadcast_to(far[1 - side : 2 - side], (8, LAYER))

                def through(number):
                    rows = jnp.broadcast_to(far[number : number + 1], (8, LAYER))
                    return pick(back, pick(rows, beyond[side]))

                ghost_y[side] = jnp.where(lower, through(3), through(2))
                ghost_z[side] = jnp.where(first_k, through(5), through(4))

        for copy in e0 + h1:
            copy.wait_recv()
        mine_dh, their_dh, their_h = [], [], []
        for side in range(2):
            sign = SIGN[side]
            outer = pick(recv_t[window, 0, side], beyond[side]) * exists[side]
            mine_dh.append(turn(outer, GAIN * sign))
            their_dh.append(turn(send_t[window, 0, side], -GAIN * sign))
            their_h.append(
                (pick(recv_t[window, 1, side], beyond[side]) + their_dh[side]) * exists[side]
            )
        pairs = ((mine_dh[0], their_dh[1]), (mine_dh[1], their_dh[0]))
        spread = []
        for at in range(2):
            high, low = halves(jnp.concatenate(pairs[at], axis=1))
            spread.append(
                jnp.dot(
                    fb_ref[at],
                    jnp.concatenate([high, high, low], axis=0),
                    preferred_element_type=f32,
                )
            )
        for side in range(2):
            for ghost in range(2):
                layer = 2 + side if ghost else side
                start = THEIRS[side] if ghost else MINE[side]
                change = their_dh[side] if ghost else mine_dh[side]
                index_y = ghost_y[side] if ghost else edge_y[side]
                index_z = ghost_z[side] if ghost else edge_z[side]
                if ghost:
                    across = send_t[window, 1, side] + mine_dh[side]
                    across = turn(across, -SIGN[side])
                    out = spread[1 - side][:, LAYER : 2 * LAYER]
                else:
                    across = turn(their_h[side], SIGN[side])
                    out = spread[side][:, 0:LAYER]
                edge = from_y(change[16:32], index_y) + from_z(change[0:16], index_z)

                def with_face(rows, extra):
                    end = start + 16
                    middle = rows[start:end] + extra
                    if start == 0:
                        return jnp.concatenate([middle, rows[end:64]], axis=0)
                    return jnp.concatenate([rows[0:start], middle], axis=0)

                speed = kick_ref[layer]
                de_ref[layer, 0:64] = -speed * with_face(out[0:64], edge)
                de_ref[layer, 64:128] = -speed * with_face(out[64:128], across[0:16])
                de_ref[layer, 128:192] = -speed * with_face(out[128:192], across[16:32])
        for n in range(2):
            e_ref[n] = e_ref[n] + de_ref[n]
            add_rows(h_ref, n, MINE[n], mine_dh[n])

        high, low = halves(jnp.concatenate([de_ref[2], de_ref[3]], axis=1))
        cuts = [tb_ref[at : at + 16, :] for at in (112, 176, 64, 128)]
        lows = [tb_ref[192 + at : 208 + at, :] for at in (112, 176, 64, 128)]
        whole = jnp.dot(jnp.concatenate(cuts + lows, axis=0), high, preferred_element_type=f32)
        rest = jnp.dot(jnp.concatenate(cuts, axis=0), low, preferred_element_type=f32)
        near = whole[0:64] + (whole[64:128] + rest)
        their_dh2 = []
        for side in range(2):
            start = THEIRS[side]
            own = de_ref[2 + side, start : start + 16]
            edge = jnp.concatenate(
                [-from_z(own, ghost_z[side]), -from_y(own, ghost_y[side])], axis=0
            )
            across = turn(rows_of(e_ref, side, MINE[side]), -SIGN[side])
            lanes = slice(side * LAYER, (side + 1) * LAYER)
            at = slice(32 * side, 32 * side + 32)
            their_dh2.append(their_dh[side] + GAIN * (near[at, lanes] + edge + across))

        fill_local(de_ref)
        for n in range(2):
            h_ref[n] = h_ref[n] + GAIN * g_ref[n]
        for copy in e1:
            copy.wait_recv()
        for side in range(2):
            outer = pick(recv_t[window, 2, side], beyond[side])
            outer = (outer + rows_of(de_ref, 2 + side, THEIRS[side])) * exists[side]
            add_rows(h_ref, side, MINE[side], turn(outer, GAIN * SIGN[side]))
        if step + 2 == STEPS:
            stores = []
            for n in range(2):
                lanes = pl.ds(n * LAYER, LAYER)
                copy = pltpu.make_async_copy(h_ref.at[n], out_h.at[0, :, lanes], store_sem.at[n])
                copy.start()
                stores.append(copy)

        add_eps(step)
        drive(step + 1)
        fill_local(h_ref)
        for n in range(2):
            e_ref[n] = e_ref[n] - kick(n)
        for copy in h2:
            copy.wait_recv()
        for side in range(2):
            outer = pick(recv_t[window, 3, side], beyond[side])
            outer = turn((outer + their_dh2[side]) * exists[side], -SIGN[side])
            speed = kick_ref[side, MINE[side] : MINE[side] + 16]
            add_rows(
                e_ref,
                side,
                MINE[side],
                jnp.concatenate([speed * outer[0:16], speed * outer[16:32]], axis=0),
            )
        if step + 2 < STEPS:
            add_eps(step + 1)

    for n in range(2):
        lanes = pl.ds(n * LAYER, LAYER)
        copy = pltpu.make_async_copy(e_ref.at[n], out_e.at[0, :, lanes], store_sem.at[2 + n])
        copy.start()
        stores.append(copy)
    add_eps(STEPS - 1)
    got_dm.wait()
    pixel = lax.broadcasted_iota(jnp.int32, (LAYER, 2 * LAYER), 0)
    members = ((dm_ref[...] & (LAYER - 1)) == pixel).astype(jnp.bfloat16)
    stacked = jnp.concatenate(
        [jnp.concatenate(sens[0], axis=1), jnp.concatenate(sens[1], axis=1)], axis=0
    )
    high, low = halves(stacked)
    contract = (((1,), (1,)), ((), ()))
    sums[...] = lax.dot_general(
        members, high, contract, preferred_element_type=f32
    ) + lax.dot_general(members, low, contract, preferred_element_type=f32)
    part_copies = []
    for hop in range(1, n_exc):
        peer = lax.rem(me_exc + hop, n_exc)
        start = pl.multiple_of(peer * own_rows, own_rows)
        copy = pltpu.make_async_remote_copy(
            src_ref=sums.at[pl.ds(start, own_rows)],
            dst_ref=parts.at[hop],
            send_sem=part_send_sem.at[hop],
            recv_sem=part_recv_sem.at[hop],
            device_id={"exc": peer},
            device_id_type=MESH,
        )
        copy.start()
        part_copies.append(copy)
    for copy in sent + once:
        copy.wait_send()
    total = sums[pl.ds(pl.multiple_of(me_exc * own_rows, own_rows), own_rows)]
    for hop in range(1, n_exc):
        part_copies[hop - 1].wait_recv()
        total = total + parts[hop]
    total = total * (1.0 / n_exc)
    out_eps[...] = total[:, 0:64]
    out_drude[...] = total[:, 64:128]
    for copy in part_copies:
        copy.wait_send()
    for copy in stores:
        copy.wait()


def write_kernel(e_in, h_in, a_in, b_in, e_out, h_out, a_out, b_out, sem):
    copies = [
        pltpu.make_async_copy(src, dst, sem.at[at])
        for at, (src, dst) in enumerate(
            ((e_in, e_out), (h_in, h_out), (a_in, a_out), (b_in, b_out))
        )
    ]
    for copy in copies:
        copy.start()
    for copy in copies:
        copy.wait()


def write(*arrays):
    spec = pl.BlockSpec(memory_space=pltpu.HBM)
    return pl.pallas_call(
        write_kernel,
        out_shape=tuple(jax.ShapeDtypeStruct(a.shape, a.dtype) for a in arrays),
        in_specs=[pl.BlockSpec(memory_space=pltpu.VMEM)] * 4,
        out_specs=(spec,) * 4,
        scratch_shapes=[pltpu.SemaphoreType.DMA((4,))],
        compiler_params=pltpu.CompilerParams(vmem_limit_bytes=2 << 20),
        name="write_out",
    )(*arrays)


def local(n_exc, n_space, *args):
    (adj_e, adj_h, adj_j, fwd_e, inv_eps, drude, neighbor, design, ports, profile) = args
    own_rows = LAYER // n_exc
    f32 = jnp.float32
    anywhere = pl.BlockSpec(memory_space=pltpu.HBM)
    in_vmem = pl.BlockSpec(memory_space=pltpu.VMEM)
    new_e, new_h, grad_eps, grad_drude = pl.pallas_call(
        functools.partial(kernel, n_exc, n_space),
        out_shape=(
            jax.ShapeDtypeStruct(adj_e.shape, f32),
            jax.ShapeDtypeStruct(adj_h.shape, f32),
            jax.ShapeDtypeStruct((own_rows, 64), f32),
            jax.ShapeDtypeStruct((own_rows, 64), f32),
        ),
        in_specs=[anywhere] * 12,
        out_specs=(anywhere, anywhere, in_vmem, in_vmem),
        scratch_shapes=[
            pltpu.VMEM((2, 192, LAYER), f32),
            pltpu.VMEM((2, 192, LAYER), f32),
            pltpu.VMEM((2, 192, LAYER), f32),
            pltpu.VMEM((2, 192, LAYER), f32),
            pltpu.VMEM((2, 192, LAYER), f32),
            pltpu.VMEM((4, 192, LAYER), f32),
            pltpu.VMEM((2, STEPS + 1, 192, LAYER), jnp.bfloat16),
            pltpu.VMEM((2, 64, LAYER), f32),
            pltpu.VMEM((2, 64, LAYER), f32),
            pltpu.VMEM((4, 64, LAYER), f32),
            pltpu.VMEM((6, 2 * LAYER), jnp.int32),
            pltpu.VMEM((1, 2 * LAYER), jnp.int32),
            pltpu.VMEM((1, LAYER), jnp.int32),
            pltpu.VMEM((192, LAYER), f32),
            pltpu.VMEM((384, 192), jnp.bfloat16),
            pltpu.VMEM((2, 192, 96), jnp.bfloat16),
            pltpu.VMEM((STEPS // 2, 4, 2, 32, LAYER), f32),
            pltpu.VMEM((STEPS // 2, 4, 2, 32, LAYER), f32),
            pltpu.VMEM((2, 64, LAYER), f32),
            pltpu.VMEM((2, 6, LAYER), jnp.int32),
            pltpu.VMEM((LAYER, LAYER), f32),
            pltpu.VMEM((n_exc, own_rows, LAYER), f32),
            pltpu.SemaphoreType.DMA((24,)),
            pltpu.SemaphoreType.DMA((STEPS // 2, 4, 2)),
            pltpu.SemaphoreType.DMA((STEPS // 2, 4, 2)),
            pltpu.SemaphoreType.DMA((2, 2)),
            pltpu.SemaphoreType.DMA((2, 2)),
            pltpu.SemaphoreType.DMA((n_exc,)),
            pltpu.SemaphoreType.DMA((n_exc,)),
            pltpu.SemaphoreType.DMA((4,)),
        ],
        compiler_params=pltpu.CompilerParams(
            collective_id=0, has_side_effects=True, vmem_limit_bytes=16 << 20
        ),
        name="adjoint_steps",
    )(
        *[pltpu.with_memory_space_constraint(x, pltpu.HBM) for x in (adj_e, adj_h, adj_j, fwd_e, inv_eps, drude, neighbor, design.reshape(1, 2 * LAYER), ports, profile, jnp.asarray(split_table()), jnp.asarray(split_faces()))]
    )
    new_e, new_h, grad_eps, grad_drude = write(new_e, new_h, grad_eps, grad_drude)
    return new_e, new_h, grad_eps.T, grad_drude.T


def solution(mesh):
    return jax.shard_map(
        functools.partial(local, mesh.shape["exc"], mesh.shape["space"]),
        mesh=mesh,
        in_specs=(
            P("exc", None, "space"),
            P("exc", None, "space"),
            P("exc", None, "space"),
            P("exc", None, None, "space"),
            P(None, "space"),
            P(None, "space"),
            P(None, "space"),
            P("space"),
            P("exc", "space"),
            P("exc", None, "space"),
        ),
        out_specs=(
            P("exc", None, "space"),
            P("exc", None, "space"),
            P(None, ("space", "exc")),
            P(None, ("space", "exc")),
        ),
        check_vma=False,
    )
```

time: 31.5 us -> 26.3 us (0.83)
  Pallas kernels: 30.7 us -> 25.5 us
    pallas_call x1, Pallas kernels: 29.9 us -> 24.7 us  [local(): pl.pallas_call(functools.partial(kernel, n_exc, n_space), out_shape=(jax....]
where the time goes in v3:
time: 26.3 us; the launch traced here: 26.1 us
  Pallas kernels  25.5 us (97%)
  between operations  0.64 us (2%)
    pallas_call x1, Pallas kernels, local(): pl.pallas_call(functools.partial(kernel, n_exc, n_space), out_shape=(jax....  24.7 us
    pallas_call x1, Pallas kernels, write(): pl.pallas_call(write_kernel, out_shape=tuple((jax.ShapeDtypeStruct(a.shap...  0.78 us

profile of v3, /device:TPU:32, one launch (start us, length us, event | category | flops | bytes accessed | tf_op | source)
XLA Modules:
  0.0 26.1 jit_solution(11107518777428226014)
XLA Ops:
  0.6 24.7 %adjoint_steps.1 = (f32[1,192,256]{2,1,0:T(8,128)S(1)}, f32[1,192,256]{2,1,0:T(8,128)S(1)}, f32[8,64]{1,0:T(8,128)S(1)}, f32[8,64]{1,0:T(8,128)S(1)}) custom-call(f32[1,192,256]{2,1,0:T(8,128)} %adj_e.1, f32[1,192,256]{2,1,0:T(8,128)} %adj_h.1, f32[1,192,256]{2,1,0:T(8,128)} %adj_j.1, bf16[1,5,192,256]{3,2,1,0:T(8,128)(2,1)} %fwd_e.1, f32[64,256]{1,0:T(8,128)} %inv_eps.1, ...), custom_call_target="tpu_custom_call" | custom-call | tf_op jit(solution)/shard_map/adjoint_steps/pallas_call | solution.py:595
  25.3 0.8 %write_out.1 = (f32[1,192,256]{2,1,0:T(8,128)}, f32[1,192,256]{2,1,0:T(8,128)}, f32[8,64]{1,0:T(8,128)}, f32[8,64]{1,0:T(8,128)}) custom-call(f32[1,192,256]{2,1,0:T(8,128)S(1)} %get-tuple-element.12.e_in, f32[1,192,256]{2,1,0:T(8,128)S(1)} %get-tuple-element.13.h_in, f32[8,64]{1,0:T(8,128)S(1)} %get-tuple-element.14.a_in, f32[8,64]{1,0:T(8,128)S(1)} %get-tuple-element.15.b_in), custom_call_target="tpu_custom_call" | custom-call | tf_op jit(solution)/shard_map/write_out/pallas_call | solution.py:578

commit v4 on v3

--- a/solution.py
+++ b/solution.py
@@ -105,6 +105,7 @@
     ref[layer, 128 + start : 144 + start] += value[16:32]
 
 
+FAR_FIRST = (10, 6, 14, 2, 9, 11, 8, 5, 7, 13, 15, 1, 3, 4, 12)
 MINE = (0, 48)
 THEIRS = (48, 0)
 SIGN = (-1.0, 1.0)
@@ -132,8 +133,12 @@
     e_ref,
     h_ref,
     j_ref,
+    level_e,
+    level_j,
+    change_ref,
+    late_ref,
     s_ref,
-    g_ref,
+    z_ref,
     de_ref,
     f_ref,
     v_ref,
@@ -170,9 +175,6 @@
     barrier = pltpu.get_barrier_semaphore()
     for peer in (left, right):
         pl.semaphore_signal(barrier, inc=1, device_id={"space": peer}, device_id_type=MESH)
-    for hop in range(1, n_exc):
-        peer = lax.rem(me_exc + hop, n_exc)
-        pl.semaphore_signal(barrier, inc=1, device_id={"exc": peer}, device_id_type=MESH)
 
     loads = []
 
@@ -198,10 +200,16 @@
     got_f = load_layers(fwd_e.at[0], f_ref)
     got_dm = load(design, dm_ref)
 
+    for hop in range(1, n_exc):
+        peer = lax.rem(me_exc + hop, n_exc)
+        pl.semaphore_signal(barrier, inc=1, device_id={"exc": peer}, device_id_type=MESH)
+
     sublane = lax.broadcasted_iota(jnp.int32, (8, LAYER), 0)
     lower = sublane < 4
     first_k = (sublane & 3) == 0
     last_k = (sublane & 3) == 3
+
+    z_ref[...] = jnp.zeros(z_ref.shape, f32)
 
     got_nb.wait()
     table_nb = nb_ref[...]
@@ -229,10 +237,23 @@
         rest = jnp.dot(tb_ref[0:192, :], low, preferred_element_type=f32)
         return whole[0:192] + (whole[192:384] + rest)
 
-    def fill_local(field_ref):
+    calls = []
+
+    def local_flux(field_ref):
         total = product(jnp.concatenate([field_ref[0], field_ref[1]], axis=1))
         zeros = jnp.zeros((48, LAYER), f32)
-        for n in range(2):
+        slot = len(calls) % 2
+        calls.append(slot)
+        result = []
+        for n in range(2):
+            far = pick(field_ref[n, pl.ds(0, 32, stride=4), :], high_z[n])
+            z_ref[slot, n, pl.ds(3, 32, stride=4), :] = jnp.concatenate(
+                [far[16:32], -far[0:16]], axis=0
+            )
+            near = pick(field_ref[n, pl.ds(3, 32, stride=4), :], low_z[n])
+            z_ref[slot, n, pl.ds(0, 32, stride=4), :] = jnp.concatenate(
+                [-near[16:32], near[0:16]], axis=0
+            )
             own = field_ref[n].reshape(3, 4, 2, 8, LAYER)
             edge = jnp.concatenate(
                 [
@@ -255,18 +276,16 @@
                 side = turn(pick(rows_of(field_ref, 0, 48), between[1]), -1.0)
                 to_y = jnp.concatenate([side[0:16], zeros], axis=0)
                 to_z2 = jnp.concatenate([side[16:32], zeros], axis=0)
-            mine = total[:, n * LAYER : (n + 1) * LAYER]
-            g_ref[n, 0:64] = mine[0:64] + to_x.reshape(64, LAYER)
-            g_ref[n, 64:128] = mine[64:128] + to_y
-            g_ref[n, 128:192] = mine[128:192] + to_z.reshape(64, LAYER) + to_z2
-            far = pick(field_ref[n, pl.ds(0, 32, stride=4), :], high_z[n])
-            g_ref[n, pl.ds(3, 32, stride=4), :] += jnp.concatenate(
-                [far[16:32], -far[0:16]], axis=0
-            )
-            near = pick(field_ref[n, pl.ds(3, 32, stride=4), :], low_z[n])
-            g_ref[n, pl.ds(0, 32, stride=4), :] += jnp.concatenate(
-                [-near[16:32], near[0:16]], axis=0
-            )
+            extra = jnp.concatenate(
+                [
+                    z_ref[slot, n, 0:64] + to_x.reshape(64, LAYER),
+                    z_ref[slot, n, 64:128] + to_y,
+                    to_z.reshape(64, LAYER) + to_z2,
+                ],
+                axis=0,
+            )
+            result.append(total[:, n * LAYER : (n + 1) * LAYER] + extra)
+        return result
 
     def from_y(rows, index):
         outer = pltpu.roll(pick(jnp.where(lower, rows[0:8], rows[8:16]), index), 4, 0)
@@ -300,10 +319,13 @@
 
     sent = []
 
-    def send_trace(window, kind, ref):
+    def keep_trace(window, kind, ref):
+        for side in range(2):
+            send_t[window, kind, side] = rows_of(ref, side, MINE[side])
+
+    def send_trace(window, kind):
         copies = []
         for side in range(2):
-            send_t[window, kind, side] = rows_of(ref, side, MINE[side])
             copies.append(
                 remote(
                     send_t.at[window, kind, side],
@@ -317,39 +339,43 @@
 
     sens = [[jnp.zeros((64, LAYER), f32)] * 2 for _ in range(2)]
 
+    def add(kind, n, field, weight):
+        term = (field * weight).reshape(3, 64, LAYER)
+        sens[kind][n] = sens[kind][n] + (term[0] + term[1] + term[2])
+
+    def change_of(n, step):
+        return f_ref[n, step + 1].astype(f32) - f_ref[n, step].astype(f32)
+
     def add_eps(step):
         for n in range(2):
-            change = f_ref[n, step + 1].astype(f32) - f_ref[n, step].astype(f32)
-            term = (e_ref[n] * change).reshape(3, 64, LAYER)
-            sens[0][n] = sens[0][n] + (term[0] + term[1] + term[2])
+            add(0, n, level_e[step, n], change_of(n, step))
+
+    def add_drude(step):
+        for n in range(2):
+            add(1, n, level_j[step, n], f_ref[n, step].astype(f32))
 
     def drive(step):
         for n in range(2):
-            electric = e_ref[n].reshape(3, 64, LAYER)
-            current = (1.0 - TIME_STEP * DAMPING) * j_ref[n].reshape(3, 64, LAYER)
-            current = current + (TIME_STEP * w_ref[n]) * electric
-            j_ref[n] = current.reshape(192, LAYER)
-            term = current * f_ref[n, step].astype(f32).reshape(3, 64, LAYER)
-            sens[1][n] = sens[1][n] + (term[0] + term[1] + term[2])
-            push = (TIME_STEP * v_ref[n]) * (current + s_ref[n].reshape(3, 64, LAYER))
+            electric = (level_e[step - 1, n] if step else e_ref[n]).reshape(3, 64, LAYER)
+            current = level_j[step - 1, n] if step else j_ref[n]
+            current = (1.0 - TIME_STEP * DAMPING) * current.reshape(3, 64, LAYER)
+            current = current + w_ref[n] * electric
+            level_j[step, n] = current.reshape(192, LAYER)
+            push = v_ref[n] * (current + s_ref[n].reshape(3, 64, LAYER))
             e_ref[n] = (electric - push).reshape(192, LAYER)
 
-    def kick(n):
-        return (kick_ref[n] * g_ref[n].reshape(3, 64, LAYER)).reshape(192, LAYER)
-
-    pl.semaphore_wait(barrier, 2 + n_exc - 1)
-    once = []
-    for side in range(2):
-        lanes = pl.ds(side * LAYER, LAYER)
-        for at, (src, dst) in enumerate(((inv_eps, recv_v), (neighbor, recv_nb))):
-            once.append(
-                remote(
-                    src.at[:, lanes],
-                    dst.at[1 - side],
-                    (once_send_sem.at[at, side], once_recv_sem.at[at, 1 - side]),
-                    side,
-                )
-            )
+    def gather_pixels(stacked):
+        pixel = lax.broadcasted_iota(jnp.int32, (LAYER, 2 * LAYER), 0)
+        members = ((dm_ref[...] & (LAYER - 1)) == pixel).astype(jnp.bfloat16)
+        high, low = halves(stacked)
+        contract = (((1,), (1,)), ((), ()))
+        return lax.dot_general(
+            members, high, contract, preferred_element_type=f32
+        ) + lax.dot_general(members, low, contract, preferred_element_type=f32)
+
+    def kick(n, flux):
+        return (kick_ref[n] * flux.reshape(3, 64, LAYER)).reshape(192, LAYER)
+
     ghost_y, ghost_z = [None, None], [None, None]
 
     for copy in got_e:
@@ -357,19 +383,39 @@
 
     for window in range(STEPS // 2):
         step = 2 * window
-        e0 = send_trace(window, 0, e_ref)
+        field = e_ref if window == 0 else level_e.at[step - 1]
+        keep_trace(window, 0, field)
+        if window > 0:
+            e0 = send_trace(window, 0)
         if window == 0:
             got_tb.wait()
-        fill_local(e_ref)
+        flux = local_flux(field)
         if window == 0:
             for copy in got_h:
                 copy.wait()
         for n in range(2):
-            h_ref[n] = h_ref[n] + GAIN * g_ref[n]
-        h1 = send_trace(window, 1, h_ref)
-
+            h_ref[n] = h_ref[n] + GAIN * flux[n]
+        keep_trace(window, 1, h_ref)
         if window == 0:
-            for copy in got_w + got_v + got_j + got_f + [got_pe, got_pp, got_fb]:
+            pl.semaphore_wait(barrier, 2 + n_exc - 1)
+            e0 = send_trace(window, 0)
+        h1 = send_trace(window, 1)
+        if window == 0:
+            once = []
+            for side in range(2):
+                lanes = pl.ds(side * LAYER, LAYER)
+                for at, (src, dst) in enumerate(((inv_eps, recv_v), (neighbor, recv_nb))):
+                    once.append(
+                        remote(
+                            src.at[:, lanes],
+                            dst.at[1 - side],
+                            (once_send_sem.at[at, side], once_recv_sem.at[at, 1 - side]),
+                            side,
+                        )
+                    )
+
+        if window == 0:
+            for copy in got_w + got_v + got_j + [got_pe, got_pp]:
                 copy.wait()
             element = lax.broadcasted_iota(jnp.int32, (2 * LAYER, LAYER), 0)
             chosen = ((pe_ref[...] & (2 * LAYER - 1)) == element).astype(jnp.bfloat16)
@@ -381,42 +427,42 @@
             for n in range(2):
                 s_ref[n] = source[:, n * LAYER : (n + 1) * LAYER]
                 kick_ref[n] = GAIN * v_ref[n]
+                v_ref[n] = TIME_STEP * v_ref[n]
+                w_ref[n] = TIME_STEP * w_ref[n]
         drive(step)
-        fill_local(h_ref)
-        for n in range(2):
-            e_ref[n] = e_ref[n] - kick(n)
-        e1 = send_trace(window, 2, e_ref)
-        fill_local(e_ref)
-        for n in range(2):
-            h_ref[n] = h_ref[n] + GAIN * g_ref[n]
-        h2 = send_trace(window, 3, h_ref)
+        flux = local_flux(h_ref)
+        for n in range(2):
+            e_ref[n] = e_ref[n] - kick(n, flux[n])
+        keep_trace(window, 2, e_ref)
+        e1 = send_trace(window, 2)
+        flux = local_flux(e_ref)
+        for n in range(2):
+            h_ref[n] = h_ref[n] + GAIN * flux[n]
+        keep_trace(window, 3, h_ref)
+        h2 = send_trace(window, 3)
 
         if window == 0:
-            for copy in once:
-                copy.wait_recv()
-            for side in range(2):
-                kick_ref[2 + side] = GAIN * pick(recv_v[side], beyond[side])
-                far = recv_nb[side] & (LAYER - 1)
-                back = jnp.broadcast_to(far[1 - side : 2 - side], (8, LAYER))
-
-                def through(number):
-                    rows = jnp.broadcast_to(far[number : number + 1], (8, LAYER))
-                    return pick(back, pick(rows, beyond[side]))
-
-                ghost_y[side] = jnp.where(lower, through(3), through(2))
-                ghost_z[side] = jnp.where(first_k, through(5), through(4))
-
-        for copy in e0 + h1:
+            for copy in got_f + [got_fb, got_dm]:
+                copy.wait()
+        add_drude(step)
+        if step + 2 < STEPS:
+            pass
+        else:
+            add_eps(step - 2)
+            add_eps(step - 1)
+            add_drude(step - 1)
+            for n in range(2):
+                for at in range(2):
+                    change_ref[at, n] = change_of(n, step + at)
+                late_ref[n] = f_ref[n, step + 1].astype(f32)
+        for copy in e0:
             copy.wait_recv()
-        mine_dh, their_dh, their_h = [], [], []
+        mine_dh, their_dh = [], []
         for side in range(2):
             sign = SIGN[side]
             outer = pick(recv_t[window, 0, side], beyond[side]) * exists[side]
             mine_dh.append(turn(outer, GAIN * sign))
             their_dh.append(turn(send_t[window, 0, side], -GAIN * sign))
-            their_h.append(
-                (pick(recv_t[window, 1, side], beyond[side]) + their_dh[side]) * exists[side]
-            )
         pairs = ((mine_dh[0], their_dh[1]), (mine_dh[1], their_dh[0]))
         spread = []
         for at in range(2):
@@ -428,58 +474,86 @@
                     preferred_element_type=f32,
                 )
             )
+
+        def respond(side, ghost, across):
+            layer = 2 + side if ghost else side
+            start = THEIRS[side] if ghost else MINE[side]
+            change = their_dh[side] if ghost else mine_dh[side]
+            index_y = ghost_y[side] if ghost else edge_y[side]
+            index_z = ghost_z[side] if ghost else edge_z[side]
+            if ghost:
+                out = spread[1 - side][:, LAYER : 2 * LAYER]
+            else:
+                out = spread[side][:, 0:LAYER]
+            edge = from_y(change[16:32], index_y) + from_z(change[0:16], index_z)
+
+            def with_face(rows, extra):
+                end = start + 16
+                middle = rows[start:end] + extra
+                if start == 0:
+                    return jnp.concatenate([middle, rows[end:64]], axis=0)
+                return jnp.concatenate([rows[0:start], middle], axis=0)
+
+            speed = kick_ref[layer]
+            de_ref[layer, 0:64] = -speed * with_face(out[0:64], edge)
+            de_ref[layer, 64:128] = -speed * with_face(out[64:128], across[0:16])
+            de_ref[layer, 128:192] = -speed * with_face(out[128:192], across[16:32])
+
+        def respond_ghosts():
+            for side in range(2):
+                across = send_t[window, 1, side] + mine_dh[side]
+                respond(side, True, turn(across, -SIGN[side]))
+
+        if window > 0:
+            respond_ghosts()
+        for copy in h1:
+            copy.wait_recv()
         for side in range(2):
-            for ghost in range(2):
-                layer = 2 + side if ghost else side
-                start = THEIRS[side] if ghost else MINE[side]
-                change = their_dh[side] if ghost else mine_dh[side]
-                index_y = ghost_y[side] if ghost else edge_y[side]
-                index_z = ghost_z[side] if ghost else edge_z[side]
-                if ghost:
-                    across = send_t[window, 1, side] + mine_dh[side]
-                    across = turn(across, -SIGN[side])
-                    out = spread[1 - side][:, LAYER : 2 * LAYER]
-                else:
-                    across = turn(their_h[side], SIGN[side])
-                    out = spread[side][:, 0:LAYER]
-                edge = from_y(change[16:32], index_y) + from_z(change[0:16], index_z)
-
-                def with_face(rows, extra):
-                    end = start + 16
-                    middle = rows[start:end] + extra
-                    if start == 0:
-                        return jnp.concatenate([middle, rows[end:64]], axis=0)
-                    return jnp.concatenate([rows[0:start], middle], axis=0)
-
-                speed = kick_ref[layer]
-                de_ref[layer, 0:64] = -speed * with_face(out[0:64], edge)
-                de_ref[layer, 64:128] = -speed * with_face(out[64:128], across[0:16])
-                de_ref[layer, 128:192] = -speed * with_face(out[128:192], across[16:32])
-        for n in range(2):
-            e_ref[n] = e_ref[n] + de_ref[n]
+            across = (pick(recv_t[window, 1, side], beyond[side]) + their_dh[side]) * exists[side]
+            respond(side, False, turn(across, SIGN[side]))
+        for n in range(2):
+            level_e[step, n] = e_ref[n] + de_ref[n]
             add_rows(h_ref, n, MINE[n], mine_dh[n])
-
-        high, low = halves(jnp.concatenate([de_ref[2], de_ref[3]], axis=1))
-        cuts = [tb_ref[at : at + 16, :] for at in (112, 176, 64, 128)]
-        lows = [tb_ref[192 + at : 208 + at, :] for at in (112, 176, 64, 128)]
-        whole = jnp.dot(jnp.concatenate(cuts + lows, axis=0), high, preferred_element_type=f32)
-        rest = jnp.dot(jnp.concatenate(cuts, axis=0), low, preferred_element_type=f32)
-        near = whole[0:64] + (whole[64:128] + rest)
-        their_dh2 = []
-        for side in range(2):
-            start = THEIRS[side]
-            own = de_ref[2 + side, start : start + 16]
-            edge = jnp.concatenate(
-                [-from_z(own, ghost_z[side]), -from_y(own, ghost_y[side])], axis=0
-            )
-            across = turn(rows_of(e_ref, side, MINE[side]), -SIGN[side])
-            lanes = slice(side * LAYER, (side + 1) * LAYER)
-            at = slice(32 * side, 32 * side + 32)
-            their_dh2.append(their_dh[side] + GAIN * (near[at, lanes] + edge + across))
-
-        fill_local(de_ref)
-        for n in range(2):
-            h_ref[n] = h_ref[n] + GAIN * g_ref[n]
+        flux = local_flux(de_ref)
+        for n in range(2):
+            h_ref[n] = h_ref[n] + GAIN * flux[n]
+
+        if window == 0:
+            for copy in once:
+                copy.wait_recv()
+            for side in range(2):
+                kick_ref[2 + side] = GAIN * pick(recv_v[side], beyond[side])
+                far = recv_nb[side] & (LAYER - 1)
+                back = jnp.broadcast_to(far[1 - side : 2 - side], (8, LAYER))
+
+                def through(number):
+                    rows = jnp.broadcast_to(far[number : number + 1], (8, LAYER))
+                    return pick(back, pick(rows, beyond[side]))
+
+                ghost_y[side] = jnp.where(lower, through(3), through(2))
+                ghost_z[side] = jnp.where(first_k, through(5), through(4))
+            respond_ghosts()
+
+        def their_second():
+            high, low = halves(jnp.concatenate([de_ref[2], de_ref[3]], axis=1))
+            cuts = [tb_ref[at : at + 16, :] for at in (112, 176, 64, 128)]
+            lows = [tb_ref[192 + at : 208 + at, :] for at in (112, 176, 64, 128)]
+            whole = jnp.dot(jnp.concatenate(cuts + lows, axis=0), high, preferred_element_type=f32)
+            rest = jnp.dot(jnp.concatenate(cuts, axis=0), low, preferred_element_type=f32)
+            near = whole[0:64] + (whole[64:128] + rest)
+            result = []
+            for side in range(2):
+                start = THEIRS[side]
+                own = de_ref[2 + side, start : start + 16]
+                edge = jnp.concatenate(
+                    [-from_z(own, ghost_z[side]), -from_y(own, ghost_y[side])], axis=0
+                )
+                across = turn(rows_of(level_e.at[step], side, MINE[side]), -SIGN[side])
+                lanes = slice(side * LAYER, (side + 1) * LAYER)
+                at = slice(32 * side, 32 * side + 32)
+                result.append(their_dh[side] + GAIN * (near[at, lanes] + edge + across))
+            return result
+
         for copy in e1:
             copy.wait_recv()
         for side in range(2):
@@ -494,11 +568,20 @@
                 copy.start()
                 stores.append(copy)
 
-        add_eps(step)
         drive(step + 1)
-        fill_local(h_ref)
-        for n in range(2):
-            e_ref[n] = e_ref[n] - kick(n)
+        flux = local_flux(h_ref)
+        for n in range(2):
+            level_e[step + 1, n] = e_ref[n] - kick(n, flux[n])
+        if step + 2 == STEPS:
+            for n in range(2):
+                add(0, n, level_e[step, n], change_ref[0, n])
+                add(1, n, level_j[step + 1, n], late_ref[n])
+            sums[...] = gather_pixels(
+                jnp.concatenate(
+                    [jnp.concatenate(sens[0], axis=1), jnp.concatenate(sens[1], axis=1)], axis=0
+                )
+            )
+        their_dh2 = their_second()
         for copy in h2:
             copy.wait_recv()
         for side in range(2):
@@ -506,33 +589,25 @@
             outer = turn((outer + their_dh2[side]) * exists[side], -SIGN[side])
             speed = kick_ref[side, MINE[side] : MINE[side] + 16]
             add_rows(
-                e_ref,
+                level_e.at[step + 1],
                 side,
                 MINE[side],
                 jnp.concatenate([speed * outer[0:16], speed * outer[16:32]], axis=0),
             )
-        if step + 2 < STEPS:
-            add_eps(step + 1)
 
     for n in range(2):
         lanes = pl.ds(n * LAYER, LAYER)
-        copy = pltpu.make_async_copy(e_ref.at[n], out_e.at[0, :, lanes], store_sem.at[2 + n])
+        copy = pltpu.make_async_copy(
+            level_e.at[STEPS - 1, n], out_e.at[0, :, lanes], store_sem.at[2 + n]
+        )
         copy.start()
         stores.append(copy)
-    add_eps(STEPS - 1)
-    got_dm.wait()
-    pixel = lax.broadcasted_iota(jnp.int32, (LAYER, 2 * LAYER), 0)
-    members = ((dm_ref[...] & (LAYER - 1)) == pixel).astype(jnp.bfloat16)
-    stacked = jnp.concatenate(
-        [jnp.concatenate(sens[0], axis=1), jnp.concatenate(sens[1], axis=1)], axis=0
-    )
-    high, low = halves(stacked)
-    contract = (((1,), (1,)), ((), ()))
-    sums[...] = lax.dot_general(
-        members, high, contract, preferred_element_type=f32
-    ) + lax.dot_general(members, low, contract, preferred_element_type=f32)
-    part_copies = []
-    for hop in range(1, n_exc):
+    sens[0] = [jnp.zeros((64, LAYER), f32)] * 2
+    for n in range(2):
+        add(0, n, level_e[STEPS - 1, n], change_ref[1, n])
+    sums[:, 0:64] += gather_pixels(jnp.concatenate(sens[0], axis=1))
+    part_copies = {}
+    for hop in FAR_FIRST if n_exc == 16 else range(1, n_exc):
         peer = lax.rem(me_exc + hop, n_exc)
         start = pl.multiple_of(peer * own_rows, own_rows)
         copy = pltpu.make_async_remote_copy(
@@ -544,17 +619,17 @@
             device_id_type=MESH,
         )
         copy.start()
-        part_copies.append(copy)
+        part_copies[hop] = copy
     for copy in sent + once:
         copy.wait_send()
     total = sums[pl.ds(pl.multiple_of(me_exc * own_rows, own_rows), own_rows)]
     for hop in range(1, n_exc):
-        part_copies[hop - 1].wait_recv()
+        part_copies[hop].wait_recv()
         total = total + parts[hop]
     total = total * (1.0 / n_exc)
     out_eps[...] = total[:, 0:64]
     out_drude[...] = total[:, 64:128]
-    for copy in part_copies:
+    for copy in part_copies.values():
         copy.wait_send()
     for copy in stores:
         copy.wait()
@@ -606,8 +681,12 @@
             pltpu.VMEM((2, 192, LAYER), f32),
             pltpu.VMEM((2, 192, LAYER), f32),
             pltpu.VMEM((2, 192, LAYER), f32),
+            pltpu.VMEM((STEPS, 2, 192, LAYER), f32),
+            pltpu.VMEM((STEPS, 2, 192, LAYER), f32),
+            pltpu.VMEM((2, 2, 192, LAYER), f32),
             pltpu.VMEM((2, 192, LAYER), f32),
             pltpu.VMEM((2, 192, LAYER), f32),
+            pltpu.VMEM((2, 2, LAYER, LAYER), f32),
             pltpu.VMEM((4, 192, LAYER), f32),
             pltpu.VMEM((2, STEPS + 1, 192, LAYER), jnp.bfloat16),
             pltpu.VMEM((2, 64, LAYER), f32),

time: 26.3 us -> 25.5 us (0.970)
  Pallas kernels: 25.5 us -> 24.8 us
    pallas_call x1, Pallas kernels: 24.7 us -> 24 us  [local(): pl.pallas_call(functools.partial(kernel, n_exc, n_space), out_shape=(jax....]
where the time goes in v4:
time: 25.5 us; the launch traced here: 25.4 us
  Pallas kernels  24.8 us (97%)
  between operations  0.64 us (3%)
    pallas_call x1, Pallas kernels, local(): pl.pallas_call(functools.partial(kernel, n_exc, n_space), out_shape=(jax....  24 us
    pallas_call x1, Pallas kernels, write(): pl.pallas_call(write_kernel, out_shape=tuple((jax.ShapeDtypeStruct(a.shap...  0.78 us

profile of v4, /device:TPU:32, one launch (start us, length us, event | category | flops | bytes accessed | tf_op | source)
XLA Modules:
  0.0 25.4 jit_solution(11695225503375408714)
XLA Ops:
  0.6 24.0 %adjoint_steps.1 = (f32[1,192,256]{2,1,0:T(8,128)S(1)}, f32[1,192,256]{2,1,0:T(8,128)S(1)}, f32[8,64]{1,0:T(8,128)S(1)}, f32[8,64]{1,0:T(8,128)S(1)}) custom-call(f32[1,192,256]{2,1,0:T(8,128)} %adj_e.1, f32[1,192,256]{2,1,0:T(8,128)} %adj_h.1, f32[1,192,256]{2,1,0:T(8,128)} %adj_j.1, bf16[1,5,192,256]{3,2,1,0:T(8,128)(2,1)} %fwd_e.1, f32[64,256]{1,0:T(8,128)} %inv_eps.1, ...), custom_call_target="tpu_custom_call" | custom-call | tf_op jit(solution)/shard_map/adjoint_steps/pallas_call | solution.py:670
  24.6 0.8 %write_out.1 = (f32[1,192,256]{2,1,0:T(8,128)}, f32[1,192,256]{2,1,0:T(8,128)}, f32[8,64]{1,0:T(8,128)}, f32[8,64]{1,0:T(8,128)}) custom-call(f32[1,192,256]{2,1,0:T(8,128)S(1)} %get-tuple-element.12.e_in, f32[1,192,256]{2,1,0:T(8,128)S(1)} %get-tuple-element.13.h_in, f32[8,64]{1,0:T(8,128)S(1)} %get-tuple-element.14.a_in, f32[8,64]{1,0:T(8,128)S(1)} %get-tuple-element.15.b_in), custom_call_target="tpu_custom_call" | custom-call | tf_op jit(solution)/shard_map/write_out/pallas_call | solution.py:653

commit v5 on v4

--- a/solution.py
+++ b/solution.py
@@ -173,8 +173,13 @@
     f32 = jnp.float32
 
     barrier = pltpu.get_barrier_semaphore()
-    for peer in (left, right):
-        pl.semaphore_signal(barrier, inc=1, device_id={"space": peer}, device_id_type=MESH)
+    has = (me_space > 0, me_space < n_space - 1)
+    for side, peer in enumerate((left, right)):
+
+        @pl.when(has[side])
+        def _():
+            pl.semaphore_signal(barrier, inc=1, device_id={"space": peer}, device_id_type=MESH)
+
 
     loads = []
 
@@ -210,6 +215,16 @@
     last_k = (sublane & 3) == 3
 
     z_ref[...] = jnp.zeros(z_ref.shape, f32)
+    for side in range(2):
+
+        @pl.when(jnp.logical_not(has[side]))
+        def _():
+            for window in range(STEPS // 2):
+                for kind in range(4):
+                    recv_t[window, kind, side] = jnp.zeros((32, LAYER), f32)
+            recv_v[side] = jnp.zeros((64, LAYER), f32)
+            recv_nb[side] = jnp.zeros((6, LAYER), jnp.int32)
+
 
     got_nb.wait()
     table_nb = nb_ref[...]
@@ -314,8 +329,20 @@
             device_id={"space": (left, right)[side]},
             device_id_type=MESH,
         )
-        copy.start()
-        return copy
+
+        @pl.when(has[side])
+        def _():
+            copy.start()
+
+        return copy, side
+
+    def arrive(copies):
+        for copy, side in copies:
+            pl.when(has[1 - side])(copy.wait_recv)
+
+    def leave(copies):
+        for copy, side in copies:
+            pl.when(has[side])(copy.wait_send)
 
     sent = []
 
@@ -397,7 +424,8 @@
             h_ref[n] = h_ref[n] + GAIN * flux[n]
         keep_trace(window, 1, h_ref)
         if window == 0:
-            pl.semaphore_wait(barrier, 2 + n_exc - 1)
+            arrivals = has[0].astype(jnp.int32) + has[1].astype(jnp.int32)
+            pl.semaphore_wait(barrier, arrivals + (n_exc - 1))
             e0 = send_trace(window, 0)
         h1 = send_trace(window, 1)
         if window == 0:
@@ -455,8 +483,7 @@
                 for at in range(2):
                     change_ref[at, n] = change_of(n, step + at)
                 late_ref[n] = f_ref[n, step + 1].astype(f32)
-        for copy in e0:
-            copy.wait_recv()
+        arrive(e0)
         mine_dh, their_dh = [], []
         for side in range(2):
             sign = SIGN[side]
@@ -506,8 +533,7 @@
 
         if window > 0:
             respond_ghosts()
-        for copy in h1:
-            copy.wait_recv()
+        arrive(h1)
         for side in range(2):
             across = (pick(recv_t[window, 1, side], beyond[side]) + their_dh[side]) * exists[side]
             respond(side, False, turn(across, SIGN[side]))
@@ -519,8 +545,7 @@
             h_ref[n] = h_ref[n] + GAIN * flux[n]
 
         if window == 0:
-            for copy in once:
-                copy.wait_recv()
+            arrive(once)
             for side in range(2):
                 kick_ref[2 + side] = GAIN * pick(recv_v[side], beyond[side])
                 far = recv_nb[side] & (LAYER - 1)
@@ -554,8 +579,7 @@
                 result.append(their_dh[side] + GAIN * (near[at, lanes] + edge + across))
             return result
 
-        for copy in e1:
-            copy.wait_recv()
+        arrive(e1)
         for side in range(2):
             outer = pick(recv_t[window, 2, side], beyond[side])
             outer = (outer + rows_of(de_ref, 2 + side, THEIRS[side])) * exists[side]
@@ -582,8 +606,7 @@
                 )
             )
         their_dh2 = their_second()
-        for copy in h2:
-            copy.wait_recv()
+        arrive(h2)
         for side in range(2):
             outer = pick(recv_t[window, 3, side], beyond[side])
             outer = turn((outer + their_dh2[side]) * exists[side], -SIGN[side])
@@ -620,8 +643,7 @@
         )
         copy.start()
         part_copies[hop] = copy
-    for copy in sent + once:
-        copy.wait_send()
+    leave(sent + once)
     total = sums[pl.ds(pl.multiple_of(me_exc * own_rows, own_rows), own_rows)]
     for hop in range(1, n_exc):
         part_copies[hop].wait_recv()

time: 25.5 us -> 25.5 us (level)
  no operation moved by 1% of the time
where the time goes in v5:
time: 25.5 us; the launch traced here: 25.3 us
  Pallas kernels  24.7 us (97%)
  between operations  0.64 us (3%)
    pallas_call x1, Pallas kernels, local(): pl.pallas_call(functools.partial(kernel, n_exc, n_space), out_shape=(jax....  23.9 us
    pallas_call x1, Pallas kernels, write(): pl.pallas_call(write_kernel, out_shape=tuple((jax.ShapeDtypeStruct(a.shap...  0.78 us

profile of v5, /device:TPU:32, one launch (start us, length us, event | category | flops | bytes accessed | tf_op | source)
XLA Modules:
  0.0 25.3 jit_solution(8034025799950533698)
XLA Ops:
  0.6 23.9 %adjoint_steps.1 = (f32[1,192,256]{2,1,0:T(8,128)S(1)}, f32[1,192,256]{2,1,0:T(8,128)S(1)}, f32[8,64]{1,0:T(8,128)S(1)}, f32[8,64]{1,0:T(8,128)S(1)}) custom-call(f32[1,192,256]{2,1,0:T(8,128)} %adj_e.1, f32[1,192,256]{2,1,0:T(8,128)} %adj_h.1, f32[1,192,256]{2,1,0:T(8,128)} %adj_j.1, bf16[1,5,192,256]{3,2,1,0:T(8,128)(2,1)} %fwd_e.1, f32[64,256]{1,0:T(8,128)} %inv_eps.1, ...), custom_call_target="tpu_custom_call" | custom-call | tf_op jit(solution)/shard_map/adjoint_steps/pallas_call | solution.py:692
  24.6 0.8 %write_out.1 = (f32[1,192,256]{2,1,0:T(8,128)}, f32[1,192,256]{2,1,0:T(8,128)}, f32[8,64]{1,0:T(8,128)}, f32[8,64]{1,0:T(8,128)}) custom-call(f32[1,192,256]{2,1,0:T(8,128)S(1)} %get-tuple-element.12.e_in, f32[1,192,256]{2,1,0:T(8,128)S(1)} %get-tuple-element.13.h_in, f32[8,64]{1,0:T(8,128)S(1)} %get-tuple-element.14.a_in, f32[8,64]{1,0:T(8,128)S(1)} %get-tuple-element.15.b_in), custom_call_target="tpu_custom_call" | custom-call | tf_op jit(solution)/shard_map/write_out/pallas_call | solution.py:675

commit v6 on v5

--- a/solution.py
+++ b/solution.py
@@ -584,14 +584,6 @@
             outer = pick(recv_t[window, 2, side], beyond[side])
             outer = (outer + rows_of(de_ref, 2 + side, THEIRS[side])) * exists[side]
             add_rows(h_ref, side, MINE[side], turn(outer, GAIN * SIGN[side]))
-        if step + 2 == STEPS:
-            stores = []
-            for n in range(2):
-                lanes = pl.ds(n * LAYER, LAYER)
-                copy = pltpu.make_async_copy(h_ref.at[n], out_h.at[0, :, lanes], store_sem.at[n])
-                copy.start()
-                stores.append(copy)
-
         drive(step + 1)
         flux = local_flux(h_ref)
         for n in range(2):
@@ -618,13 +610,6 @@
                 jnp.concatenate([speed * outer[0:16], speed * outer[16:32]], axis=0),
             )
 
-    for n in range(2):
-        lanes = pl.ds(n * LAYER, LAYER)
-        copy = pltpu.make_async_copy(
-            level_e.at[STEPS - 1, n], out_e.at[0, :, lanes], store_sem.at[2 + n]
-        )
-        copy.start()
-        stores.append(copy)
     sens[0] = [jnp.zeros((64, LAYER), f32)] * 2
     for n in range(2):
         add(0, n, level_e[STEPS - 1, n], change_ref[1, n])
@@ -643,6 +628,15 @@
         )
         copy.start()
         part_copies[hop] = copy
+    stores = []
+    for n in range(2):
+        lanes = pl.ds(n * LAYER, LAYER)
+        for at, (src, dst) in enumerate(((h_ref, out_h), (level_e.at[STEPS - 1], out_e))):
+            copy = pltpu.make_async_copy(
+                src.at[n], dst.at[0, :, lanes], store_sem.at[2 * at + n]
+            )
+            copy.start()
+            stores.append(copy)
     leave(sent + once)
     total = sums[pl.ds(pl.multiple_of(me_exc * own_rows, own_rows), own_rows)]
     for hop in range(1, n_exc):

time: 25.5 us -> 25.4 us (level)
  no operation moved by 1% of the time
where the time goes in v6:
time: 25.4 us; the launch traced here: 25.3 us
  Pallas kernels  24.6 us (97%)
  between operations  0.64 us (3%)
    pallas_call x1, Pallas kernels, local(): pl.pallas_call(functools.partial(kernel, n_exc, n_space), out_shape=(jax....  23.8 us
    pallas_call x1, Pallas kernels, write(): pl.pallas_call(write_kernel, out_shape=tuple((jax.ShapeDtypeStruct(a.shap...  0.78 us

profile of v6, /device:TPU:32, one launch (start us, length us, event | category | flops | bytes accessed | tf_op | source)
XLA Modules:
  0.0 25.3 jit_solution(4078683800594189029)
XLA Ops:
  0.6 23.8 %adjoint_steps.1 = (f32[1,192,256]{2,1,0:T(8,128)S(1)}, f32[1,192,256]{2,1,0:T(8,128)S(1)}, f32[8,64]{1,0:T(8,128)S(1)}, f32[8,64]{1,0:T(8,128)S(1)}) custom-call(f32[1,192,256]{2,1,0:T(8,128)} %adj_e.1, f32[1,192,256]{2,1,0:T(8,128)} %adj_h.1, f32[1,192,256]{2,1,0:T(8,128)} %adj_j.1, bf16[1,5,192,256]{3,2,1,0:T(8,128)(2,1)} %fwd_e.1, f32[64,256]{1,0:T(8,128)} %inv_eps.1, ...), custom_call_target="tpu_custom_call" | custom-call | tf_op jit(solution)/shard_map/adjoint_steps/pallas_call | solution.py:686
  24.5 0.8 %write_out.1 = (f32[1,192,256]{2,1,0:T(8,128)}, f32[1,192,256]{2,1,0:T(8,128)}, f32[8,64]{1,0:T(8,128)}, f32[8,64]{1,0:T(8,128)}) custom-call(f32[1,192,256]{2,1,0:T(8,128)S(1)} %get-tuple-element.12.e_in, f32[1,192,256]{2,1,0:T(8,128)S(1)} %get-tuple-element.13.h_in, f32[8,64]{1,0:T(8,128)S(1)} %get-tuple-element.14.a_in, f32[8,64]{1,0:T(8,128)S(1)} %get-tuple-element.15.b_in), custom_call_target="tpu_custom_call" | custom-call | tf_op jit(solution)/shard_map/write_out/pallas_call | solution.py:669

commit v7 on v5

--- a/solution.py
+++ b/solution.py
@@ -172,6 +172,11 @@
     own_rows = LAYER // n_exc
     f32 = jnp.float32
 
+    def around(hop):
+        if n_exc & (n_exc - 1) == 0:
+            return (me_exc + hop) & (n_exc - 1)
+        return lax.rem(me_exc + hop, n_exc)
+
     barrier = pltpu.get_barrier_semaphore()
     has = (me_space > 0, me_space < n_space - 1)
     for side, peer in enumerate((left, right)):
@@ -206,7 +211,7 @@
     got_dm = load(design, dm_ref)
 
     for hop in range(1, n_exc):
-        peer = lax.rem(me_exc + hop, n_exc)
+        peer = around(hop)
         pl.semaphore_signal(barrier, inc=1, device_id={"exc": peer}, device_id_type=MESH)
 
     sublane = lax.broadcasted_iota(jnp.int32, (8, LAYER), 0)
@@ -631,7 +636,7 @@
     sums[:, 0:64] += gather_pixels(jnp.concatenate(sens[0], axis=1))
     part_copies = {}
     for hop in FAR_FIRST if n_exc == 16 else range(1, n_exc):
-        peer = lax.rem(me_exc + hop, n_exc)
+        peer = around(hop)
         start = pl.multiple_of(peer * own_rows, own_rows)
         copy = pltpu.make_async_remote_copy(
             src_ref=sums.at[pl.ds(start, own_rows)],

time: 25.5 us -> 25.5 us (level)
  no operation moved by 1% of the time
where the time goes in v7:
time: 25.5 us; the launch traced here: 25.3 us
  Pallas kernels  24.7 us (97%)
  between operations  0.64 us (3%)
    pallas_call x1, Pallas kernels, local(): pl.pallas_call(functools.partial(kernel, n_exc, n_space), out_shape=(jax....  23.9 us
    pallas_call x1, Pallas kernels, write(): pl.pallas_call(write_kernel, out_shape=tuple((jax.ShapeDtypeStruct(a.shap...  0.78 us

profile of v7, /device:TPU:32, one launch (start us, length us, event | category | flops | bytes accessed | tf_op | source)
XLA Modules:
  0.0 25.3 jit_solution(17285727578468410937)
XLA Ops:
  0.6 23.9 %adjoint_steps.1 = (f32[1,192,256]{2,1,0:T(8,128)S(1)}, f32[1,192,256]{2,1,0:T(8,128)S(1)}, f32[8,64]{1,0:T(8,128)S(1)}, f32[8,64]{1,0:T(8,128)S(1)}) custom-call(f32[1,192,256]{2,1,0:T(8,128)} %adj_e.1, f32[1,192,256]{2,1,0:T(8,128)} %adj_h.1, f32[1,192,256]{2,1,0:T(8,128)} %adj_j.1, bf16[1,5,192,256]{3,2,1,0:T(8,128)(2,1)} %fwd_e.1, f32[64,256]{1,0:T(8,128)} %inv_eps.1, ...), custom_call_target="tpu_custom_call" | custom-call | tf_op jit(solution)/shard_map/adjoint_steps/pallas_call | solution.py:697
  24.5 0.8 %write_out.1 = (f32[1,192,256]{2,1,0:T(8,128)}, f32[1,192,256]{2,1,0:T(8,128)}, f32[8,64]{1,0:T(8,128)}, f32[8,64]{1,0:T(8,128)}) custom-call(f32[1,192,256]{2,1,0:T(8,128)S(1)} %get-tuple-element.12.e_in, f32[1,192,256]{2,1,0:T(8,128)S(1)} %get-tuple-element.13.h_in, f32[8,64]{1,0:T(8,128)S(1)} %get-tuple-element.14.a_in, f32[8,64]{1,0:T(8,128)S(1)} %get-tuple-element.15.b_in), custom_call_target="tpu_custom_call" | custom-call | tf_op jit(solution)/shard_map/write_out/pallas_call | solution.py:680
